TPU v7x, 32 devices: a whole 2x2x4 slice. The times are simulated.
32 devices in a mesh: dp: 4 (over y, x), seq: 8 (over z, core).
Axes of the slice: x: 2, y: 2, z: 4, core: 2. Of those that a mesh axis runs over, the one named last changes fastest.
Arguments:
- inputs: float32 [3, 4, 1024, 2048], P(None, 'dp', 'seq'), may hold values from -6 to 6
- segment_ids: int32 [3, 4, 1024], P(None, 'dp', 'seq'), may hold values from 0 to 7, never falling along the last dimension, each value on 1 to 512 neighbouring positions
- cotangent: float32 [3, 4, 1024, 2048], P(None, 'dp', 'seq'), may hold values from -6 to 6
- mixer_gain: bfloat16 [2048], P(('dp', 'seq')), may hold values from 0.099609375 to 1.8984375
- input_proj: bfloat16 [2048, 2048], P(('dp', 'seq')), may hold values from -0.125 to 0.125
- forget_proj: bfloat16 [2048, 2048], P(('dp', 'seq')), may hold values from -0.125 to 0.125
- gate_proj: bfloat16 [2048, 2048], P(('dp', 'seq')), may hold values from -0.125 to 0.125
- floor_log: bfloat16 [2048], P(('dp', 'seq')), may hold values from -12 to -2
- output_gain: bfloat16 [2048], P(('dp', 'seq')), may hold values from 0.099609375 to 1.8984375
- output_proj: bfloat16 [2048, 2048], P(('dp', 'seq')), may hold values from -0.25 to 0.25
- dense_gain: bfloat16 [2048], P(('dp', 'seq')), may hold values from 0.099609375 to 1.8984375
- up_first: bfloat16 [2048, 5632], P(('dp', 'seq')), may hold values from -0.125 to 0.125
- up_second: bfloat16 [2048, 5632], P(('dp', 'seq')), may hold values from -0.125 to 0.125
- down_proj: bfloat16 [5632, 2048], P(('dp', 'seq')), may hold values from -0.15625 to 0.15625
Outputs:
- block_out: float32 [3, 4, 1024, 2048], P(None, 'dp', 'seq')
- input_grad: float32 [3, 4, 1024, 2048], P(None, 'dp', 'seq')
- mixer_gain_grad: float32 [2048], P(('dp', 'seq'))
- input_proj_grad: float32 [2048, 2048], P(('dp', 'seq'))
- forget_proj_grad: float32 [2048, 2048], P(('dp', 'seq'))
- gate_proj_grad: float32 [2048, 2048], P(('dp', 'seq'))
- floor_log_grad: float32 [2048], P(('dp', 'seq'))
- output_gain_grad: float32 [2048], P(('dp', 'seq'))
- output_proj_grad: float32 [2048, 2048], P(('dp', 'seq'))
- dense_gain_grad: float32 [2048], P(('dp', 'seq'))
- up_first_grad: float32 [2048, 5632], P(('dp', 'seq'))
- up_second_grad: float32 [2048, 5632], P(('dp', 'seq'))
- down_proj_grad: float32 [5632, 2048], P(('dp', 'seq'))
Inputs may be any that keep to these rules, and one draw needn't show every extreme that they name: `segment_ids`: along each sequence the document numbers never fall; each document spans at most 512 tokens, and one spans exactly that many.
All inputs are finite; a program needn't handle non-finite values.
Results may differ from a plain program's by a relative error of at most 0.012.
Values may be sent and summed in bfloat16 or wider, within the bound.
A program may use at most 512 MiB of HBM per device.

v0:
```python
import jax
import jax.numpy as jnp
from jax import lax
from jax.sharding import PartitionSpec as P

norm_eps = 1e-06


def prefix(x, axis, combine, identity):
    devices, index = (lax.axis_size(axis), lax.axis_index(axis))
    everything = jax.tree.map(
        lambda part, kind: lax.all_gather(part.astype(kind), axis),
        x,
        (jnp.bfloat16, jnp.bfloat16, jnp.bfloat16, jnp.bfloat16),
    )
    start = jax.tree.map(
        lambda part, zero: jnp.broadcast_to(jnp.asarray(zero, part.dtype), part.shape), x, identity
    )

    def lap(k, before):
        reached = k < index
        new = combine(
            before, jax.tree.map(lambda part, own: part[k].astype(own.dtype), everything, x)
        )
        return jax.tree.map(lambda a, b: jnp.where(reached, a, b), new, before)

    return lax.fori_loop(0, devices, lap, start)


def entering_2(x, axis, join, neutral):
    count = lax.axis_size(axis)
    place = lax.axis_index(axis)
    ahead = count - 1 - place
    gathered = jax.tree.map(
        lambda a, kind: lax.all_gather(a.astype(kind), axis),
        x,
        jax.tree.map(lambda a: jnp.bfloat16 if a.dtype == jnp.float32 else a.dtype, x),
    )
    state = jax.tree.map(lambda a, e: jnp.zeros_like(a) + jnp.asarray(e, a.dtype), x, neutral)

    def one(lap, state):
        source = count - 1 - lap
        return join(
            state,
            jax.tree.map(
                lambda a, own: lax.dynamic_index_in_dim(a, source, 0, False).astype(own.dtype),
                gathered,
                x,
            ),
        )

    return lax.fori_loop(0, ahead, one, state)


def silu_slope(values):
    logistic = jax.nn.sigmoid(values)
    return logistic * (1.0 + values * (1.0 - logistic))


def norm_back(upstream, scaled, factor):
    return factor * (upstream - scaled * jnp.mean(upstream * scaled, axis=-1, keepdims=True))


def affine_pairs(earlier, later):
    decay_one, state_one = earlier
    decay_two, state_two = later
    return (decay_one * decay_two, decay_two * state_one + state_two)


def settle(earlier, later, merged):
    early_empty = earlier[0] < 0.0
    late_empty = later[0] < 0.0
    outcome = []
    for member_early, member_late, member_merged in zip(earlier, later, merged):
        if member_merged.ndim == 2:
            mask_early = early_empty[:, None]
            mask_late = late_empty[:, None]
        else:
            mask_early = early_empty
            mask_late = late_empty
        outcome.append(
            jnp.where(mask_early, member_late, jnp.where(mask_late, member_early, member_merged))
        )
    return tuple(outcome)


def chain_forward(earlier, later):
    head_early, tail_early, decay_early, state_early = earlier
    head_late, tail_late, decay_late, state_late = later
    linked = (head_late == tail_early).astype(jnp.float32)[:, None]
    carried = decay_late * linked
    merged = (head_early, tail_late, carried * decay_early, carried * state_early + state_late)
    return settle(earlier, later, merged)


def chain_backward(earlier, later):
    head_early, tail_early, mult_early, acc_early = earlier
    head_late, tail_late, mult_late, acc_late = later
    linked = (head_early == tail_late).astype(jnp.float32)[:, None]
    carried = mult_late * linked
    merged = (head_late, tail_early, carried * mult_early, carried * acc_early + acc_late)
    return settle(earlier, later, merged)


def contract_last(left, right):
    return lax.dot_general(
        left, right, (((1,), (1,)), ((), ())), preferred_element_type=jnp.float32
    )


def contract_rows(left, right):
    return lax.dot_general(
        left, right, (((0,), (0,)), ((), ())), preferred_element_type=jnp.float32
    )


def shards(
    inputs,
    segment_ids,
    cotangent,
    mixer_gain,
    input_proj,
    forget_proj,
    gate_proj,
    floor_log,
    output_gain,
    output_proj,
    dense_gain,
    up_first,
    up_second,
    down_proj,
):
    width = inputs.shape[-1]
    hidden_units = up_first.shape[1]
    groups = inputs.shape[0] * inputs.shape[1]
    span_len = inputs.shape[2]
    rows_all = groups * span_len
    flat = inputs.reshape(rows_all, width)
    scale_one = lax.rsqrt(jnp.mean(flat * flat, axis=1, keepdims=True) + norm_eps)
    scaled_one = flat * scale_one
    whole_gain, whole_input, whole_forget, whole_gate, floor_whole = (
        lax.all_gather(mixer_gain, ("dp", "seq"), axis=0, tiled=True),
        lax.all_gather(input_proj, ("dp", "seq"), axis=0, tiled=True),
        lax.all_gather(forget_proj, ("dp", "seq"), axis=0, tiled=True),
        lax.all_gather(gate_proj, ("dp", "seq"), axis=0, tiled=True),
        lax.all_gather(floor_log, ("dp", "seq"), axis=0, tiled=True),
    )
    normed_one = (scaled_one * whole_gain.astype(jnp.float32)).astype(jnp.bfloat16)
    pre_input = jnp.dot(normed_one, whole_input, preferred_element_type=jnp.float32)
    pre_forget = jnp.dot(normed_one, whole_forget, preferred_element_type=jnp.float32)
    pre_gate = jnp.dot(normed_one, whole_gate, preferred_element_type=jnp.float32)
    floor_full = floor_whole.astype(jnp.float32)
    gate_input = jax.nn.silu(pre_input)
    leak = jnp.exp(floor_full) * jax.nn.sigmoid(-pre_forget)
    forget_seq = (1.0 - leak).reshape(groups, span_len, width)
    seg_rows = segment_ids.reshape(groups, span_len)
    linked_inner = (seg_rows[:, 1:] == seg_rows[:, :-1]).astype(jnp.float32)
    decay = jnp.concatenate(
        [forget_seq[:, :1], forget_seq[:, 1:] * linked_inner[:, :, None]], axis=1
    )
    inflow = (leak * gate_input).reshape(groups, span_len, width)
    products, partial_state = lax.associative_scan(affine_pairs, (decay, inflow), axis=1)
    head_seg = seg_rows[:, 0].astype(jnp.float32)
    tail_seg = seg_rows[:, -1].astype(jnp.float32)
    empty_ids = jnp.full((groups,), -1.0, jnp.float32)
    empty_state = jnp.zeros((groups, width), jnp.float32)
    incoming = prefix(
        (head_seg, tail_seg, products[:, -1], partial_state[:, -1]),
        "seq",
        chain_forward,
        (empty_ids, empty_ids, empty_state, empty_state),
    )
    entering = incoming[3] * (incoming[1] == head_seg).astype(jnp.float32)[:, None]
    states = products * entering[:, None, :] + partial_state
    states_flat = states.reshape(rows_all, width)
    state_scale = lax.rsqrt(jnp.mean(states_flat * states_flat, axis=1, keepdims=True) + norm_eps)
    normed_state = states_flat * state_scale
    gate_out = jax.nn.silu(pre_gate)
    gathered = (
        lax.all_gather(output_gain, ("dp", "seq"), axis=0, tiled=True),
        lax.all_gather(output_proj, ("dp", "seq"), axis=0, tiled=True),
        lax.all_gather(dense_gain, ("dp", "seq"), axis=0, tiled=True),
        lax.all_gather(up_first, ("dp", "seq"), axis=0, tiled=True),
        lax.all_gather(up_second, ("dp", "seq"), axis=0, tiled=True),
        lax.all_gather(down_proj, ("dp", "seq"), axis=0, tiled=True),
    )
    out_gain_full, out_proj_full, dense_gain_full, first_full, second_full, down_full = gathered
    out_gain_float = out_gain_full.astype(jnp.float32)
    dense_gain_float = dense_gain_full.astype(jnp.float32)
    mixed_kept = (normed_state * out_gain_float * gate_out).astype(jnp.bfloat16)
    middle = flat + jnp.dot(mixed_kept, out_proj_full, preferred_element_type=jnp.float32)
    scale_two = lax.rsqrt(jnp.mean(middle * middle, axis=1, keepdims=True) + norm_eps)
    scaled_two = middle * scale_two
    normed_two = (scaled_two * dense_gain_float).astype(jnp.bfloat16)
    up_one = jnp.dot(normed_two, first_full, preferred_element_type=jnp.float32)
    up_two = jnp.dot(normed_two, second_full, preferred_element_type=jnp.float32)
    activated = (jax.nn.silu(up_one) * up_two).astype(jnp.bfloat16)
    block_out = (
        middle + jnp.dot(activated, down_full, preferred_element_type=jnp.float32)
    ).reshape(inputs.shape)
    back_weights = (
        lax.all_gather(output_gain, ("dp", "seq"), axis=0, tiled=True),
        lax.all_gather(output_proj, ("dp", "seq"), axis=0, tiled=True),
        lax.all_gather(dense_gain, ("dp", "seq"), axis=0, tiled=True),
        lax.all_gather(up_first, ("dp", "seq"), axis=0, tiled=True),
        lax.all_gather(up_second, ("dp", "seq"), axis=0, tiled=True),
        lax.all_gather(down_proj, ("dp", "seq"), axis=0, tiled=True),
    )
    back_out_gain, back_out_proj, back_dense_gain, back_first, back_second, back_down = back_weights
    back_out_gain_float = back_out_gain.astype(jnp.float32)
    back_dense_float = back_dense_gain.astype(jnp.float32)
    grad_flat = cotangent.reshape(rows_all, width)
    grad_dense = grad_flat.astype(jnp.bfloat16)
    grad_act = contract_last(grad_dense, back_down)
    grad_up_one = (grad_act * up_two * silu_slope(up_one)).astype(jnp.bfloat16)
    grad_up_two = (grad_act * jax.nn.silu(up_one)).astype(jnp.bfloat16)
    grad_normed_two = contract_last(grad_up_one, back_first) + contract_last(
        grad_up_two, back_second
    )
    gain_two = jnp.sum(grad_normed_two * scaled_two, axis=0)
    grad_middle = grad_flat + norm_back(grad_normed_two * back_dense_float, scaled_two, scale_two)
    grad_mixer = grad_middle.astype(jnp.bfloat16)
    grad_mix_in = contract_last(grad_mixer, back_out_proj)
    gain_out = jnp.sum(grad_mix_in * normed_state * gate_out, axis=0)
    grad_pre_gate = (
        grad_mix_in * normed_state * back_out_gain_float * silu_slope(pre_gate)
    ).astype(jnp.bfloat16)
    grad_normed_state = grad_mix_in * back_out_gain_float * gate_out
    grad_states = norm_back(grad_normed_state, normed_state, state_scale).reshape(
        groups, span_len, width
    )
    shifted = jnp.concatenate([decay[:, 1:], jnp.ones((groups, 1, width), jnp.float32)], axis=1)
    reverse_mult, reverse_grad = lax.associative_scan(
        affine_pairs, (jnp.flip(shifted, 1), jnp.flip(grad_states, 1)), axis=1
    )
    carry_mult = jnp.flip(reverse_mult, 1)
    local_grad = jnp.flip(reverse_grad, 1)
    outgoing = entering_2(
        (head_seg, tail_seg, decay[:, 0] * carry_mult[:, 0], decay[:, 0] * local_grad[:, 0]),
        "seq",
        chain_backward,
        (empty_ids, empty_ids, empty_state, empty_state),
    )
    arriving = outgoing[3] * (outgoing[0] == tail_seg).astype(jnp.float32)[:, None]
    adjoint = (local_grad + carry_mult * arriving[:, None, :]).reshape(rows_all, width)
    previous = jnp.concatenate(
        [entering[:, None, :], states[:, :-1] * linked_inner[:, :, None]], axis=1
    )
    grad_forget = adjoint * (previous.reshape(rows_all, width) - gate_input)
    grad_pre_input = (adjoint * leak * silu_slope(pre_input)).astype(jnp.bfloat16)
    grad_pre_forget = (grad_forget * leak * jax.nn.sigmoid(pre_forget)).astype(jnp.bfloat16)
    floor_sum = -jnp.sum(grad_forget * leak, axis=0)
    back_gain, back_input, back_forget, back_gate = (
        lax.all_gather(mixer_gain, ("dp", "seq"), axis=0, tiled=True),
        lax.all_gather(input_proj, ("dp", "seq"), axis=0, tiled=True),
        lax.all_gather(forget_proj, ("dp", "seq"), axis=0, tiled=True),
        lax.all_gather(gate_proj, ("dp", "seq"), axis=0, tiled=True),
    )
    block_all = (
        contract_last(grad_pre_input, back_input)
        + contract_last(grad_pre_forget, back_forget)
        + contract_last(grad_pre_gate, back_gate)
    )
    grad_scaled_one = block_all * back_gain.astype(jnp.float32)
    gain_one = jnp.sum(block_all * scaled_one, axis=0)
    input_grad = (grad_middle + norm_back(grad_scaled_one, scaled_one, scale_one)).reshape(
        inputs.shape
    )
    weight_terms = lax.psum_scatter(
        jnp.concatenate(
            [
                contract_rows(normed_one, grad_pre_input),
                contract_rows(normed_one, grad_pre_forget),
                contract_rows(normed_one, grad_pre_gate),
                contract_rows(mixed_kept, grad_mixer),
                contract_rows(normed_two, grad_up_one),
                contract_rows(normed_two, grad_up_two),
            ],
            axis=1,
        ),
        ("dp", "seq"),
        scatter_dimension=0,
        tiled=True,
    )
    down_proj_grad = lax.psum_scatter(
        contract_rows(activated, grad_dense), ("dp", "seq"), scatter_dimension=0, tiled=True
    )
    gain_sums = (
        lax.psum_scatter(gain_one, ("dp", "seq"), scatter_dimension=0, tiled=True),
        lax.psum_scatter(gain_out, ("dp", "seq"), scatter_dimension=0, tiled=True),
        lax.psum_scatter(gain_two, ("dp", "seq"), scatter_dimension=0, tiled=True),
        lax.psum_scatter(floor_sum, ("dp", "seq"), scatter_dimension=0, tiled=True),
    )
    input_proj_grad = weight_terms[:, :width]
    forget_proj_grad = weight_terms[:, width : 2 * width]
    gate_proj_grad = weight_terms[:, 2 * width : 3 * width]
    output_proj_grad = weight_terms[:, 3 * width : 4 * width]
    up_first_grad = weight_terms[:, 4 * width : 4 * width + hidden_units]
    up_second_grad = weight_terms[:, 4 * width + hidden_units :]
    return (
        block_out,
        input_grad,
        gain_sums[0],
        input_proj_grad,
        forget_proj_grad,
        gate_proj_grad,
        gain_sums[3],
        gain_sums[1],
        output_proj_grad,
        gain_sums[2],
        up_first_grad,
        up_second_grad,
        down_proj_grad,
    )


def solution(mesh):
    placed = (
        P(None, "dp", "seq", None),
        P(None, "dp", "seq"),
        P(None, "dp", "seq", None),
        P(("dp", "seq")),
        P(("dp", "seq"), None),
        P(("dp", "seq"), None),
        P(("dp", "seq"), None),
        P(("dp", "seq")),
        P(("dp", "seq")),
        P(("dp", "seq"), None),
        P(("dp", "seq")),
        P(("dp", "seq"), None),
        P(("dp", "seq"), None),
        P(("dp", "seq"), None),
    )
    return jax.shard_map(
        shards,
        mesh=mesh,
        in_specs=placed,
        out_specs=(
            P(None, "dp", "seq", None),
            P(None, "dp", "seq", None),
            P(("dp", "seq")),
            P(("dp", "seq"), None),
            P(("dp", "seq"), None),
            P(("dp", "seq"), None),
            P(("dp", "seq")),
            P(("dp", "seq")),
            P(("dp", "seq"), None),
            P(("dp", "seq")),
            P(("dp", "seq"), None),
            P(("dp", "seq"), None),
            P(("dp", "seq"), None),
        ),
        check_vma=False,
    )
```

profile of v0, /device:TPU:0, one launch (start us, length us, event | category | flops | bytes accessed | tf_op | source)
XLA Modules:
  0.0 3314.4 jit_solution(6307993687448192442)
XLA Ops:
  13.9 18.2 all-reduce.70
  33.8 38.9 %all-reduce.69 = (bf16[2048]{0:T(1024)(128)(2,1)S(1)}, bf16[2048]{0:T(1024)(128)(2,1)S(1)}, bf16[2048]{0:T(1024)(128)(2,1)S(1)}, bf16[2048]{0:T(1024)(128)(2,1)S(1)}) all-reduce(bf16[2048]{0:T(1024)(128)(2,1)S(1)} %dynamic-update-slice.1, bf16[2048]{0:T(1024)(128)(2,1)S(1)} %dynamic-update-slice, ...), channel_id=1, replica_groups=mesh['dp'=4,'seq'=8] {'dp','seq'}, use_global_device_ids=true, to_apply=%add.59 | all-reduce | flops 8192 | bytes 32768
  80.3 12.2 all-gather.16.cloned.1.call-done
  100.9 70.4 %all-gather.14.cloned.1.call-done = bf16[2048,2048]{1,0:T(8,128)(2,1)} async-done(((bf16[64,2048]{1,0:T(8,128)(2,1)}), bf16[2048,2048]{1,0:T(8,128)(2,1)}) %all-gather.14.cloned.1.call-update) | async-done | bytes 8388624 | tf_op jit(solution)/shard_map/all_gather | solution.py:144
  171.3 10.0 broadcast_subtract_fusion
  385.2 14.6 all-gather.3
  406.9 14.8 all-gather.2
  429.2 9.5 slice.552
  438.7 9.5 slice.543
  460.7 9.2 multiply_convert_fusion.6
  481.4 16.4 fusion.70
  497.9 124.4 %all-gather.22.cloned.1.call-done = bf16[2048,5632]{1,0:T(8,128)(2,1)} async-done(((bf16[64,5632]{1,0:T(8,128)(2,1)}), bf16[2048,5632]{1,0:T(8,128)(2,1)}) %all-gather.22.cloned.1.call-update) | async-done | bytes 23068688 | tf_op jit(solution)/shard_map/all_gather | solution.py:183
  622.3 15.7 fusion.69
  638.0 130.0 %all-gather.26.cloned.1.call-done = bf16[5632,2048]{1,0:T(8,128)(2,1)} async-done(((bf16[176,2048]{1,0:T(8,128)(2,1)}), bf16[5632,2048]{1,0:T(8,128)(2,1)}) %all-gather.26.cloned.1.call-update) | async-done | bytes 23068688 | tf_op jit(solution)/shard_map/all_gather | solution.py:185
  768.0 23.4 multiply_convert_fusion
  791.4 16.0 fusion.71
  807.4 18.5 multiply_reduce_fusion
  831.5 9.9 multiply_reduce_fusion.1
  979.8 24.8 rev.10
  1004.6 24.5 rev.9
  1029.1 14.1 all-gather.5
  1043.8 14.1 all-gather.4
  1082.7 8.7 convolution_dynamic-update-slice_fusion.4
  1099.6 8.7 convolution_dynamic-update-slice_fusion.2
  1108.3 21.1 convolution_dynamic-update-slice_fusion.1
  1129.4 20.9 convolution_dynamic-update-slice_fusion
  1151.8 21.1 fusion.74
  1185.3 9.3 multiply_reduce_fusion.2
  1194.6 39.5 %all-reduce.68 = (f32[2048]{0:T(1024)S(1)}, f32[2048]{0:T(1024)S(1)}, f32[2048]{0:T(1024)S(1)}, f32[2048]{0:T(1024)S(1)}) all-reduce(f32[2048]{0:T(1024)S(1)} %get-tuple-element.402, f32[2048]{0:T(1024)S(1)} %neg.27, f32[2048]{0:T(1024)S(1)} %copy-done.83, f32[2048]{0:T(1024)S(1)} %copy-done.82), channel_id=8, replica_groups=mesh['dp'=4,'seq'=8] {'dp','seq'}, use_global_device_ids=true, to_apply=%region_11.12.clone | all-reduce | flops 8192 | bytes 65536
  1242.8 16.0 convolution_add_fusion.1
  1258.9 1557.3 %reduce-scatter.3.cloned.1.call-done = f32[64,19456]{1,0:T(8,128)} async-done(((f32[2048,19456]{1,0:T(8,128)}), f32[64,19456]{1,0:T(8,128)}) %reduce-scatter.3.cloned.1.call-update) | async-done | bytes 4980752 | tf_op jit(solution)/shard_map/reduce_scatter | solution.py:269
  2822.7 484.9 %reduce-scatter.5.cloned.1.call-done = f32[176,2048]{1,0:T(8,128)} async-done(((f32[5632,2048]{1,0:T(8,128)}), f32[176,2048]{1,0:T(8,128)}) %reduce-scatter.5.cloned.1.call-update) | async-done | bytes 1441808 | tf_op jit(solution)/shard_map/reduce_scatter | solution.py:285
  (543 shorter events, 482.7 us)
Async XLA Ops:
  7.2 25.7 copy-start.87
  7.2 25.9 copy-start.88
  7.2 26.1 copy-start.89
  7.2 26.4 copy-start.90
  7.2 85.2 %all-gather.16.cloned.1.call-start = ((), (), s32[]{:S(2)}) async-start(), calls=%async_computation.3 | async-start | bytes 8650752 | tf_op jit(solution)/shard_map/all_gather | solution.py:143
  8.0 163.4 %all-gather.14.cloned.1.call-start = ((), (), s32[]{:S(2)}) async-start(), calls=%async_computation.2 | async-start | bytes 8650752 | tf_op jit(solution)/shard_map/all_gather | solution.py:144
  8.7 451.9 %all-gather.18.cloned.1.call-start = ((), (), s32[]{:S(2)}) async-start(), calls=%async_computation.4 | async-start | bytes 8650752 | tf_op jit(solution)/shard_map/all_gather | solution.py:145
  9.5 460.5 %all-gather.20.cloned.1.call-start = ((), (), s32[]{:S(2)}) async-start(), calls=%async_computation.5 | async-start | bytes 8650752 | tf_op jit(solution)/shard_map/all_gather | solution.py:181
  10.0 471.4 %all-gather.24.cloned.1.call-start = ((), (), s32[]{:S(2)}) async-start(), calls=%async_computation.7 | async-start | bytes 23789568 | tf_op jit(solution)/shard_map/all_gather | solution.py:184
  10.6 611.6 %all-gather.22.cloned.1.call-start = ((), (), s32[]{:S(2)}) async-start(), calls=%async_computation.6 | async-start | bytes 23789568 | tf_op jit(solution)/shard_map/all_gather | solution.py:183
  11.2 756.8 %all-gather.26.cloned.1.call-start = ((), (), s32[]{:S(2)}) async-start(), calls=%async_computation.8 | async-start | bytes 23789568 | tf_op jit(solution)/shard_map/all_gather | solution.py:185
  11.9 2804.2 %reduce-scatter.3.cloned.1.call-start = ((), (), s32[]{:S(2)}) async-start(), calls=%async_computation.9 | async-start | bytes 164364288 | tf_op jit(solution)/shard_map/reduce_scatter | solution.py:269
  74.1 133.4 %copy-start.78 = (f32[3,127]{1,0:T(4,128)}, f32[3,127]{1,0:T(4,128)S(1)}, u32[]{:S(2)}) copy-start(f32[3,127]{1,0:T(4,128)S(1)} %fusion.45) | copy-start | bytes 4576
  76.4 95.0 %copy-start.75 = (f32[2048]{0:T(1024)}, f32[2048]{0:T(1024)S(1)}, u32[]{:S(2)}) copy-start(f32[2048]{0:T(1024)S(1)} %convert_exponential_fusion) | copy-start | bytes 24580
  80.3 380.4 %copy-start = (bf16[384,2048]{1,0:T(8,128)(2,1)}, bf16[384,2048]{1,0:T(8,128)(2,1)S(1)}, u32[]{:S(2)}) copy-start(bf16[384,2048]{1,0:T(8,128)(2,1)S(1)} %multiply_convert_fusion.7) | copy-start | bytes 4718596
  207.5 19.3 copy-start.56
  376.4 24.0 copy-start.32
  385.2 37.1 %copy-start.55 = (f32[3,2048]{1,0:T(4,128)S(1)}, f32[3,2048]{1,0:T(4,128)}, u32[]{:S(2)}) copy-start(f32[3,2048]{1,0:T(4,128)} %custom-call.2) | copy-start | bytes 73732
  385.2 37.1 %copy-start.74 = (f32[3]{0:T(128)S(1)}, f32[3]{0:T(128)}, u32[]{:S(2)}) copy-start(f32[3]{0:T(128)} %custom-call) | copy-start | bytes 40
  400.5 28.6 copy-start.86
  429.1 19.1 copy-start.72
  429.2 19.0 copy-start.27
  481.4 140.9 %copy-start.9 = (bf16[384,2048]{1,0:T(8,128)(2,1)}, bf16[384,2048]{1,0:T(8,128)(2,1)S(1)}, u32[]{:S(2)}) copy-start(bf16[384,2048]{1,0:T(8,128)(2,1)S(1)} %multiply_convert_fusion.5) | copy-start | bytes 4718596
  497.9 270.1 %copy-start.39 = (bf16[384,2048]{1,0:T(8,128)(2,1)S(1)}, bf16[384,2048]{1,0:T(8,128)(2,1)}, u32[]{:S(2)}) copy-start(bf16[384,2048]{1,0:T(8,128)(2,1)} %bitcast_convert_fusion) | copy-start | bytes 4718596
  830.5 10.9 copy-start.6
  900.6 10.5 copy-start.31
  1004.6 53.9 %copy-start.73 = (bf16[8,3]{1,0:T(8,128)(2,1)S(1)}, bf16[8,3]{1,0:T(8,128)(2,1)}, u32[]{:S(2)}) copy-start(bf16[8,3]{1,0:T(8,128)(2,1)} %copy-done.72) | copy-start | bytes 148
  1004.6 59.4 %copy-start.85 = (f32[3]{0:T(128)S(1)}, f32[3]{0:T(128)}, u32[]{:S(2)}) copy-start(f32[3]{0:T(128)} %get-tuple-element.404) | copy-start | bytes 40
  1073.8 8.9 copy-start.37
  1150.4 2157.2 %reduce-scatter.5.cloned.1.call-start = ((), (), s32[]{:S(2)}) async-start(), calls=%async_computation.10 | async-start | bytes 47579136 | tf_op jit(solution)/shard_map/reduce_scatter | solution.py:285
  1185.2 9.3 copy-start.82
  1185.3 9.3 copy-start.83
  (69 other events, 306.0 us)
Sparse Core Ops, SparseCore 0:
  11.1 81.3 all-gather.15
  95.4 75.8 all-gather.13
  174.3 75.9 all-gather.17
  253.2 76.0 all-gather.19
  332.0 144.7 all-gather.23
  479.4 142.8 all-gather.21
  625.1 142.7 all-gather.25
  1150.5 1665.5 reduce-scatter.2
  2819.1 488.4 reduce-scatter.4
where the time goes:
time: 3330 us; the launch traced here: 3310 us
  waiting for transfers between devices  2380 us (71%)
  local copies, waits for them, and re-layouts  357 us (11%)
  matrix products  271 us (8%)
  blocking collectives  154 us (5%)
  other arithmetic  131 us (4%)
    reduce_scatter x1, waiting for transfers between devices, shards(): lax.psum_scatter(jnp.concatenate([contract_rows(normed_one, grad_pre_inpu...  1560 us
    reduce_scatter x1, waiting for transfers between devices, shards(): lax.psum_scatter(contract_rows(activated, grad_dense), ('dp', 'seq'), sca...  485 us
    all_gather x1, waiting for transfers between devices, shards(): lax.all_gather(down_proj, ('dp', 'seq'), axis=0, tiled=True)  130 us
    all_gather x1, waiting for transfers between devices, shards(): lax.all_gather(up_first, ('dp', 'seq'), axis=0, tiled=True)  124 us
    slice x49, local copies, waits for them, and re-layouts, shards(): lax.associative_scan(affine_pairs, (jnp.flip(shifted, 1), jnp.flip(grad_s...  110 us
    dot_general x7, matrix products, contract_rows(): lax.dot_general(left, right, (((0,), (0,)), ((), ())), preferred_element_...  97.1 us
    unnamed x3, blocking collectives  96.6 us
    dot_general x7, matrix products, contract_last(): lax.dot_general(left, right, (((1,), (1,)), ((), ())), preferred_element_...  89.4 us
  transfers between devices with their start and end apart: 9, of which 6 were waited for; matrix products, arithmetic and copies ran while one was open for 12% of the time, Pallas kernels for 0%

commit v1 on v0

v1 whole, which is shorter than its diff:
```python
import jax
import jax.numpy as jnp
from jax import lax
from jax.experimental import pallas as pl
from jax.experimental.pallas import tpu as pltpu
from jax.sharding import PartitionSpec as P

norm_eps = 1e-06
ALL = ("dp", "seq")
LANES = 128
SUB = 8


def silu_slope(values):
    logistic = jax.nn.sigmoid(values)
    return logistic * (1.0 + values * (1.0 - logistic))


def norm_back(upstream, scaled, factor):
    return factor * (upstream - scaled * jnp.mean(upstream * scaled, axis=-1, keepdims=True))


def dot(left, right):
    return jnp.dot(left, right, preferred_element_type=jnp.float32)


def contract_last(left, right):
    return lax.dot_general(
        left, right, (((1,), (1,)), ((), ())), preferred_element_type=jnp.float32
    )


def contract_rows(left, right):
    return lax.dot_general(
        left, right, (((0,), (0,)), ((), ())), preferred_element_type=jnp.float32
    )


def shift_down(values, amount, fill):
    rows = lax.broadcasted_iota(jnp.int32, values.shape, 0)
    return jnp.where(rows < amount, fill, pltpu.roll(values, amount, 0))


def shift_up(values, amount, fill):
    rows = lax.broadcasted_iota(jnp.int32, values.shape, 0)
    return jnp.where(
        rows >= SUB - amount, fill, pltpu.roll(values, SUB - amount, 0)
    )


def forward_scan_kernel(span_len, pre_input, pre_forget, floor, link, products, partial):
    tiles = span_len // SUB
    scale = jnp.exp(floor[...].astype(jnp.float32))
    width = pre_input.shape[1]
    groups = pre_input.shape[0] // span_len

    def group(g, _):
        def tile(i, carry):
            prod_in, state_in = carry
            rows = pl.ds(pl.multiple_of(g * span_len + i * SUB, SUB), SUB)
            value = pre_input[rows, :]
            leak = scale * jax.nn.sigmoid(-pre_forget[rows, :])
            decay = (1.0 - leak) * link[rows, :1]
            state = leak * value * jax.nn.sigmoid(value)
            for step in (1, 2, 4):
                state = decay * shift_down(state, step, 0.0) + state
                decay = decay * shift_down(decay, step, 1.0)
            state = decay * state_in + state
            decay = decay * prod_in
            products[rows, :] = decay
            partial[rows, :] = state
            return decay[SUB - 1 :, :], state[SUB - 1 :, :]

        lax.fori_loop(
            0, tiles, tile, (jnp.ones((1, width), jnp.float32), jnp.zeros((1, width), jnp.float32))
        )
        return 0

    lax.fori_loop(0, groups, group, 0)


def backward_scan_kernel(span_len, grad_states, pre_forget, floor, link, local, carry_mult, head):
    tiles = span_len // SUB
    scale = jnp.exp(floor[...].astype(jnp.float32))
    width = grad_states.shape[1]
    groups = grad_states.shape[0] // span_len

    def group(g, _):
        def tile(k, carry):
            prod_in, pass_in = carry
            i = tiles - 1 - k
            rows = pl.ds(pl.multiple_of(g * span_len + i * SUB, SUB), SUB)
            upstream = grad_states[rows, :]
            decay = (1.0 - scale * jax.nn.sigmoid(-pre_forget[rows, :])) * link[rows, :1]
            passed = decay * upstream
            for step in (1, 2, 4):
                passed = decay * shift_up(passed, step, 0.0) + passed
                decay = decay * shift_up(decay, step, 1.0)
            passed = decay * pass_in + passed
            decay = decay * prod_in
            local[rows, :] = upstream + shift_up(passed, 1, pass_in)
            carry_mult[rows, :] = shift_up(decay, 1, prod_in)
            return decay[:1, :], passed[:1, :]

        prod_out, pass_out = lax.fori_loop(
            0, tiles, tile, (jnp.ones((1, width), jnp.float32), jnp.zeros((1, width), jnp.float32))
        )
        head[pl.ds(g, 1), :] = pass_out
        return 0

    lax.fori_loop(0, groups, group, 0)


def scan_block(width):
    return 256 if width % 256 == 0 else width


def forward_scan(pre_all, floor, link, span_len, width):
    rows = pre_all.shape[0]
    block = scan_block(width)
    steps = width // block
    out = jax.ShapeDtypeStruct((rows, width), jnp.float32)
    return pl.pallas_call(
        lambda *refs: forward_scan_kernel(span_len, *refs),
        grid=(steps,),
        in_specs=[
            pl.BlockSpec((rows, block), lambda j: (0, j)),
            pl.BlockSpec((rows, block), lambda j: (0, j + steps)),
            pl.BlockSpec((1, block), lambda j: (0, j)),
            pl.BlockSpec((rows, LANES), lambda j: (0, 0)),
        ],
        out_specs=[pl.BlockSpec((rows, block), lambda j: (0, j))] * 2,
        out_shape=[out, out],
    )(pre_all, pre_all, floor, link)


def backward_scan(grad_states, pre_all, floor, link, span_len, width):
    rows = pre_all.shape[0]
    groups = rows // span_len
    block = scan_block(width)
    steps = width // block
    out = jax.ShapeDtypeStruct((rows, width), jnp.float32)
    return pl.pallas_call(
        lambda *refs: backward_scan_kernel(span_len, *refs),
        grid=(steps,),
        in_specs=[
            pl.BlockSpec((rows, block), lambda j: (0, j)),
            pl.BlockSpec((rows, block), lambda j: (0, j + steps)),
            pl.BlockSpec((1, block), lambda j: (0, j)),
            pl.BlockSpec((rows, LANES), lambda j: (0, 0)),
        ],
        out_specs=[pl.BlockSpec((rows, block), lambda j: (0, j))] * 2
        + [pl.BlockSpec((groups, block), lambda j: (0, j))],
        out_shape=[out, out, jax.ShapeDtypeStruct((groups, width), jnp.float32)],
    )(grad_states, pre_all, floor, link)


def entering_forward(mult, value):
    parts, place = lax.axis_size("seq"), lax.axis_index("seq")
    both = lax.all_gather(jnp.stack([mult, value]).astype(jnp.bfloat16), "seq").astype(jnp.float32)
    total = jnp.zeros_like(value)
    for k in range(parts - 1):
        total = jnp.where(k < place, both[k, 0] * total + both[k, 1], total)
    return total


def entering_backward(mult, value):
    parts, place = lax.axis_size("seq"), lax.axis_index("seq")
    both = lax.all_gather(jnp.stack([mult, value]).astype(jnp.bfloat16), "seq").astype(jnp.float32)
    total = jnp.zeros_like(value)
    for k in range(parts - 1, 0, -1):
        total = jnp.where(k > place, both[k, 0] * total + both[k, 1], total)
    return total


def gather_all(shard):
    return lax.all_gather(shard, ALL, axis=0, tiled=True)


def scatter_all(whole):
    return lax.psum_scatter(whole, ALL, scatter_dimension=0, tiled=True)


def shards(
    inputs,
    segment_ids,
    cotangent,
    mixer_gain,
    input_proj,
    forget_proj,
    gate_proj,
    floor_log,
    output_gain,
    output_proj,
    dense_gain,
    up_first,
    up_second,
    down_proj,
):
    width = inputs.shape[-1]
    hidden = up_first.shape[1]
    groups = inputs.shape[0] * inputs.shape[1]
    span_len = inputs.shape[2]
    rows_all = groups * span_len
    parts, place = lax.axis_size("seq"), lax.axis_index("seq")

    vectors = jnp.stack([mixer_gain, floor_log, output_gain, dense_gain], axis=1)
    vectors = jnp.pad(vectors, ((0, 0), (0, LANES - 4)))
    mix_full = gather_all(
        jnp.concatenate([input_proj, forget_proj, gate_proj, vectors], axis=1)
    )
    out_full = gather_all(output_proj)
    up_full = gather_all(jnp.concatenate([up_first, up_second], axis=1))
    down_full = gather_all(down_proj)
    gains = mix_full[:, 3 * width : 3 * width + 4].T
    mixer_gain_all = gains[0:1].astype(jnp.float32)
    floor_all = gains[1:2].astype(jnp.float32)
    out_gain_all = gains[2:3].astype(jnp.float32)
    dense_gain_all = gains[3:4].astype(jnp.float32)

    seg = segment_ids.reshape(groups, span_len)
    before = lax.ppermute(seg[:, -1:], "seq", [(i, i + 1) for i in range(parts - 1)])
    before = jnp.where(place == 0, -1, before)
    link = (seg == jnp.concatenate([before, seg[:, :-1]], axis=1)).astype(jnp.float32)
    link = jnp.broadcast_to(link.reshape(rows_all, 1), (rows_all, LANES))

    flat = inputs.reshape(rows_all, width)
    scale_one = lax.rsqrt(jnp.mean(flat * flat, axis=1, keepdims=True) + norm_eps)
    scaled_one = flat * scale_one
    normed_one = (scaled_one * mixer_gain_all).astype(jnp.bfloat16)
    pre_all = dot(normed_one, mix_full)
    pre_input = pre_all[:, :width]
    pre_forget = pre_all[:, width : 2 * width]
    pre_gate = pre_all[:, 2 * width : 3 * width]

    products, partial_state = forward_scan(pre_all, floor_all, link, span_len, width)
    products = products.reshape(groups, span_len, width)
    span_mult = products[:, -1]
    entering = entering_forward(
        span_mult, partial_state.reshape(groups, span_len, width)[:, -1]
    )
    states = products * entering[:, None, :] + partial_state.reshape(groups, span_len, width)
    states_flat = states.reshape(rows_all, width)
    state_scale = lax.rsqrt(jnp.mean(states_flat * states_flat, axis=1, keepdims=True) + norm_eps)
    normed_state = states_flat * state_scale
    gate_out = jax.nn.silu(pre_gate)
    mixed = (normed_state * out_gain_all * gate_out).astype(jnp.bfloat16)
    middle = flat + dot(mixed, out_full)
    scale_two = lax.rsqrt(jnp.mean(middle * middle, axis=1, keepdims=True) + norm_eps)
    scaled_two = middle * scale_two
    normed_two = (scaled_two * dense_gain_all).astype(jnp.bfloat16)
    up_both = dot(normed_two, up_full)
    up_one, up_two = up_both[:, :hidden], up_both[:, hidden:]
    activated = (jax.nn.silu(up_one) * up_two).astype(jnp.bfloat16)
    block_out = (middle + dot(activated, down_full)).reshape(inputs.shape)

    grad_flat = cotangent.reshape(rows_all, width)
    grad_dense = grad_flat.astype(jnp.bfloat16)
    grad_act = contract_last(grad_dense, down_full)
    grad_up = jnp.concatenate(
        [
            (grad_act * up_two * silu_slope(up_one)).astype(jnp.bfloat16),
            (grad_act * jax.nn.silu(up_one)).astype(jnp.bfloat16),
        ],
        axis=1,
    )
    grad_normed_two = contract_last(grad_up, up_full)
    gain_two = jnp.sum(grad_normed_two * scaled_two, axis=0)
    grad_middle = grad_flat + norm_back(grad_normed_two * dense_gain_all, scaled_two, scale_two)
    grad_mixer = grad_middle.astype(jnp.bfloat16)
    grad_mix_in = contract_last(grad_mixer, out_full)
    gain_out = jnp.sum(grad_mix_in * normed_state * gate_out, axis=0)
    grad_pre_gate = (
        grad_mix_in * normed_state * out_gain_all * silu_slope(pre_gate)
    ).astype(jnp.bfloat16)
    grad_states = norm_back(grad_mix_in * out_gain_all * gate_out, normed_state, state_scale)

    local_grad, carry_mult, head_grad = backward_scan(
        grad_states, pre_all, floor_all, link, span_len, width
    )
    arriving = entering_backward(span_mult, head_grad)
    adjoint = (
        local_grad.reshape(groups, span_len, width)
        + carry_mult.reshape(groups, span_len, width) * arriving[:, None, :]
    ).reshape(rows_all, width)
    previous = jnp.concatenate([entering[:, None, :], states[:, :-1]], axis=1)
    previous = previous.reshape(rows_all, width) * link[:, :1]
    leak = jnp.exp(floor_all) * jax.nn.sigmoid(-pre_forget)
    grad_forget = adjoint * (previous - jax.nn.silu(pre_input))
    grad_pre_input = (adjoint * leak * silu_slope(pre_input)).astype(jnp.bfloat16)
    grad_pre_forget = (grad_forget * leak * jax.nn.sigmoid(pre_forget)).astype(jnp.bfloat16)
    floor_sum = -jnp.sum(grad_forget * leak, axis=0)
    grad_pre = jnp.concatenate(
        [
            grad_pre_input,
            grad_pre_forget,
            grad_pre_gate,
            jnp.zeros((rows_all, LANES), jnp.bfloat16),
        ],
        axis=1,
    )
    block_all = contract_last(grad_pre, mix_full)
    gain_one = jnp.sum(block_all * scaled_one, axis=0)
    input_grad = (
        grad_middle + norm_back(block_all * mixer_gain_all, scaled_one, scale_one)
    ).reshape(inputs.shape)

    low = jnp.bfloat16
    vector_sums = jnp.stack([gain_one, floor_sum, gain_out, gain_two], axis=1)
    terms = scatter_all(
        jnp.concatenate(
            [
                contract_rows(normed_one, grad_pre[:, : 3 * width]).astype(low),
                contract_rows(mixed, grad_mixer).astype(low),
                contract_rows(normed_two, grad_up).astype(low),
                jnp.pad(vector_sums, ((0, 0), (0, LANES - 4))).astype(low),
            ],
            axis=1,
        )
    ).astype(jnp.float32)
    down_grad = scatter_all(contract_rows(activated, grad_dense).astype(low)).astype(jnp.float32)
    base = 4 * width + 2 * hidden
    return (
        block_out,
        input_grad,
        terms[:, base],
        terms[:, :width],
        terms[:, width : 2 * width],
        terms[:, 2 * width : 3 * width],
        terms[:, base + 1],
        terms[:, base + 2],
        terms[:, 3 * width : 4 * width],
        terms[:, base + 3],
        terms[:, 4 * width : 4 * width + hidden],
        terms[:, 4 * width + hidden : base],
        down_grad,
    )


def solution(mesh):
    whole = P(None, "dp", "seq", None)
    vector = P(ALL)
    matrix = P(ALL, None)
    return jax.shard_map(
        shards,
        mesh=mesh,
        in_specs=(
            whole,
            P(None, "dp", "seq"),
            whole,
            vector,
            matrix,
            matrix,
            matrix,
            vector,
            vector,
            matrix,
            vector,
            matrix,
            matrix,
            matrix,
        ),
        out_specs=(
            whole,
            whole,
            vector,
            matrix,
            matrix,
            matrix,
            vector,
            vector,
            matrix,
            vector,
            matrix,
            matrix,
            matrix,
        ),
        check_vma=False,
    )
```

time: 3330 us -> 1670 us (0.50)
  waiting for transfers between devices: 2380 us -> 1170 us
  local copies, waits for them, and re-layouts: 357 us -> 27.2 us
  blocking collectives: 154 us -> 29.9 us
  Pallas kernels: 0 us -> 70.3 us
    reduce_scatter x2, waiting for transfers between devices: 2040 us -> 662 us  [scatter_all(): return lax.psum_scatter(whole, ALL, scatter_dimension=0, tiled=True)]
    slice x95 -> x7, local copies, waits for them, and re-layouts: 197 us -> 7.8 us  [the longest x1 1.87 us: shards(): gains = mix_full[:, 3 * width:3 * width + 4].T]
    all_gather x7 -> x4, waiting for transfers between devices: 337 us -> 511 us  [gather_all(): return lax.all_gather(shard, ALL, axis=0, tiled=True)]
    unnamed x3 -> x0, blocking collectives: 96.6 us -> none
    pad x48 -> x0, local copies, waits for them, and re-layouts: 90.9 us -> none  [the longest x24 55.2 us: shards(): lax.associative_scan(affine_pairs, (decay, inflow), axis=1)]
    pallas_call x0 -> x2, Pallas kernels: none -> 70.3 us  [the longest x1 36.4 us: backward_scan(): pl.pallas_call(lambda *refs: backward_scan_kernel(span_len, *refs), grid=...]
    rev x2 -> x0, local copies, waits for them, and re-layouts: 49.3 us -> none  [the longest x1 24.8 us: shards(): carry_mult = jnp.flip(reverse_mult, 1)]
    concatenate x24 -> x4, other arithmetic: 23.1 us -> 58.8 us  [the longest x1 52.2 us: shards(): jnp.concatenate([contract_rows(normed_one, grad_pre[:, :3 * width]).astyp...]
  transfers between devices with their start and end apart: 9 -> 7, of which waited for: 6 -> 4; matrix products, arithmetic and copies ran while one was open for 12% -> 19% of each run, Pallas kernels for 0% -> 4%
where the time goes in v1:
time: 1670 us; the launch traced here: 1660 us
  waiting for transfers between devices  1170 us (70%)
  matrix products  239 us (14%)
  other arithmetic  107 us (6%)
  Pallas kernels  70.3 us (4%)
  blocking collectives  29.9 us (2%)
  local copies, waits for them, and re-layouts  27.2 us (2%)
    reduce_scatter x2, waiting for transfers between devices, scatter_all(): return lax.psum_scatter(whole, ALL, scatter_dimension=0, tiled=True)  662 us
    all_gather x4, waiting for transfers between devices, gather_all(): return lax.all_gather(shard, ALL, axis=0, tiled=True)  511 us
    dot_general x4, matrix products, contract_rows(): lax.dot_general(left, right, (((0,), (0,)), ((), ())), preferred_element_...  81.5 us
    dot_general x4, matrix products, contract_last(): lax.dot_general(left, right, (((1,), (1,)), ((), ())), preferred_element_...  80.4 us
    dot_general x4, matrix products, dot(): return jnp.dot(left, right, preferred_element_type=jnp.float32)  76.8 us
    concatenate x1, other arithmetic, shards(): jnp.concatenate([contract_rows(normed_one, grad_pre[:, :3 * width]).astyp...  52.2 us
    pallas_call x1, Pallas kernels, backward_scan(): pl.pallas_call(lambda *refs: backward_scan_kernel(span_len, *refs), grid=...  36.4 us
    pallas_call x1, Pallas kernels, forward_scan(): pl.pallas_call(lambda *refs: forward_scan_kernel(span_len, *refs), grid=(...  33.9 us
  transfers between devices with their start and end apart: 7, of which 4 were waited for; matrix products, arithmetic and copies ran while one was open for 19% of the time, Pallas kernels for 4%

profile of v1, /device:TPU:0, one launch (start us, length us, event | category | flops | bytes accessed | tf_op | source)
XLA Modules:
  0.0 1664.9 jit_solution(12159750097127721362)
XLA Ops:
  10.9 2.7 pad_maximum_fusion.4
  20.1 151.2 %all-gather.5.cloned.1.call-done = bf16[2048,6272]{1,0:T(8,128)(2,1)} async-done(((bf16[64,6272]{1,0:T(8,128)(2,1)}), bf16[2048,6272]{1,0:T(8,128)(2,1)}) %all-gather.5.cloned.1.call-update) | async-done | bytes 25690128 | tf_op jit(solution)/shard_map/all_gather | solution.py:177
  175.4 18.4 %fusion.75.refs_0_.refs_1_ = f32[384,6272]{1,0:T(8,128)} fusion(bf16[384,2048]{1,0:T(8,128)(2,1)S(1)} %multiply_convert_fusion.8, bf16[2048,6272]{1,0:T(8,128)(2,1)} %all-gather.5.cloned.1.call-done), kind=kOutput, calls=%fused_computation.188 | convolution fusion | flops 9865003008 | bytes 36896768 | tf_op jit(solution)/shard_map/dot_general | solution.py:24
  194.6 33.9 %shard_map.237 = (f32[384,2048]{1,0:T(8,128)}, f32[384,2048]{1,0:T(8,128)}) custom-call(f32[384,6272]{1,0:T(8,128)} %fusion.75.refs_0_.refs_1_, f32[384,6272]{1,0:T(8,128)} %fusion.75.refs_0_.refs_1_, f32[1,2048]{1,0:T(1,128)} %get-tuple-element.107.refs_2_, f32[384,128]{1,0:T(8,128)} %broadcast_in_dim.9.refs_3_), custom_call_target="tpu_custom_call" | custom-call | tf_op jit(solution)/shard_map/pallas_call | solution.py:123
  231.1 14.7 all_gather.21
  246.8 3.5 multiply_reduce_fusion.7
  250.3 4.0 multiply_convert_fusion.7
  254.3 9.8 multiply_reduce_fusion.6
  264.1 243.9 %all-gather.9.cloned.1.call-done = bf16[2048,11264]{1,0:T(8,128)(2,1)} async-done(((bf16[64,11264]{1,0:T(8,128)(2,1)}), bf16[2048,11264]{1,0:T(8,128)(2,1)}) %all-gather.9.cloned.1.call-update) | async-done | bytes 46137360 | tf_op jit(solution)/shard_map/all_gather | solution.py:177
  508.0 29.4 %fusion.68 = f32[384,11264]{1,0:T(8,128)} fusion(bf16[2048,11264]{1,0:T(8,128)(2,1)} %all-gather.9.cloned.1.call-done, f32[384,2048]{1,0:T(8,128)} %get-tuple-element.110, f32[2048]{0:T(1024)S(1)} %bitcast.436, f32[384]{0:T(512)S(1)} %add_rsqrt_fusion), kind=kOutput, calls=%fused_computation.184 | convolution fusion | flops 17719099392 | bytes 66594304 | tf_op jit(solution)/shard_map/dot_general | solution.py:24
  537.4 116.2 %all-gather.11.cloned.1.call-done = bf16[5632,2048]{1,0:T(8,128)(2,1)} async-done(((bf16[176,2048]{1,0:T(8,128)(2,1)}), bf16[5632,2048]{1,0:T(8,128)(2,1)}) %all-gather.11.cloned.1.call-update) | async-done | bytes 23068688 | tf_op jit(solution)/shard_map/all_gather | solution.py:177
  653.6 23.9 %multiply_convert_fusion.1 = (bf16[384,5632]{1,0:T(8,128)(2,1)}, bf16[384,5632]{1,0:T(8,128)(2,1)}, bf16[384,5632]{1,0:T(8,128)(2,1)}) fusion(f32[384,11264]{1,0:T(8,128)} %fusion.68, bf16[384,2048]{1,0:T(8,128)(2,1)} %bitcast_convert_fusion, bf16[5632,2048]{1,0:T(8,128)(2,1)} %all-gather.11.cloned.1.call-done), kind=kOutput, calls=%fused_computation.8 | convolution fusion | flops 8890810368 | bytes 54919168 | tf_op jit(solution)/shard_map/dot_general | solution.py:28
  677.5 19.1 %convolution_convert_fusion.1 = bf16[5632,2048]{1,0:T(8,128)(2,1)} fusion(bf16[384,5632]{1,0:T(8,128)(2,1)} %get-tuple-element.93, bf16[384,2048]{1,0:T(8,128)(2,1)} %bitcast_convert_fusion), kind=kOutput, calls=%fused_computation.4 | convolution fusion | flops 8869904384 | bytes 28966912 | tf_op jit(solution)/shard_map/dot_general | solution.py:34
  698.6 3.9 slice_add_fusion
  704.5 27.9 %multiply_reduce_fusion = (bf16[2048]{0:T(1024)(128)(2,1)S(1)}, f32[384]{0:T(512)S(1)}, f32[384,2048]{1,0:T(8,128)}) fusion(f32[384,2048]{1,0:T(8,128)} %get-tuple-element.110, f32[384]{0:T(512)S(1)} %add_rsqrt_fusion, f32[2048]{0:T(1024)S(1)} %bitcast.437, bf16[2048,11264]{1,0:T(8,128)(2,1)} %all-gather.9.cloned.1.call-done, ...), kind=kOutput, calls=%fused_computation.41 | convolution fusion | flops 17738758144 | bytes 61094912 | tf_op jit(solution)/shard_map/dot_general | solution.py:28
  732.5 4.6 bitcast_add_fusion
  737.1 9.9 multiply_reduce_fusion.1
  747.0 5.1 subtract_multiply_fusion
  752.1 36.4 %shard_map.238 = (f32[384,2048]{1,0:T(8,128)}, f32[384,2048]{1,0:T(8,128)}, f32[3,2048]{1,0:T(4,128)}) custom-call(f32[384,2048]{1,0:T(8,128)} %get-tuple-element.95.refs_0_, f32[384,6272]{1,0:T(8,128)} %fusion.75.refs_0_.refs_1_, f32[1,2048]{1,0:T(1,128)} %get-tuple-element.107.refs_2_, f32[384,128]{1,0:T(8,128)} %broadcast_in_dim.9.refs_3_), custom_call_target="tpu_custom_call" | custom-call | tf_op jit(solution)/shard_map/pallas_call | solution.py:143
  789.3 15.2 all_gather.25
  804.7 7.4 fusion.69
  812.1 4.1 multiply_convert_fusion.4
  816.2 18.7 %multiply_reduce_fusion.2 = (bf16[2048]{0:T(1024)(128)(2,1)S(1)}, f32[384]{0:T(512)S(1)}, f32[384,2048]{1,0:T(8,128)}) fusion(f32[3,1,128,2048]{3,2,1,0:T(8,128)S(1)} %copy-done.1, f32[384]{0:T(512)S(1)} %copy-done.14, f32[2048]{0:T(1024)S(1)} %bitcast.433, bf16[2048,6272]{1,0:T(8,128)(2,1)} %all-gather.5.cloned.1.call-done, ...), kind=kOutput, calls=%fused_computation.43 | convolution fusion | flops 9888987136 | bytes 36728064 | tf_op jit(solution)/shard_map/dot_general | solution.py:28
  836.0 10.2 convolution_convert_fusion.3
  846.2 12.3 copy.77
  858.6 19.8 %convolution_convert_fusion.2 = bf16[2048,6144]{1,0:T(8,128)(2,1)} fusion(bf16[384,2048]{1,0:T(8,128)(2,1)} %copy-done.8, bf16[384,2048]{1,0:T(8,128)(2,1)} %get-tuple-element.96, bf16[384,2048]{1,0:T(8,128)(2,1)} %multiply_convert_fusion.4, bf16[384,2048]{1,0:T(8,128)(2,1)} %get-tuple-element.94), kind=kOutput, calls=%fused_computation.5 | convolution fusion | flops 9690415104 | bytes 31457280 | tf_op jit(solution)/shard_map/dot_general | solution.py:34
  878.3 32.5 %convolution_convert_fusion = bf16[2048,11264]{1,0:T(8,128)(2,1)} fusion(bf16[384,5632]{1,0:T(8,128)(2,1)} %get-tuple-element.92, bf16[384,5632]{1,0:T(8,128)(2,1)} %get-tuple-element.91, f32[384,2048]{1,0:T(8,128)} %get-tuple-element.110, f32[2048]{0:T(1024)S(1)} %bitcast.439, f32[384]{0:T(512)S(1)} %add_rsqrt_fusion), kind=kOutput, calls=%fused_computation.3 | convolution fusion | flops 17759469568 | bytes 57943552 | tf_op jit(solution)/shard_map/dot_general | solution.py:34
  910.8 52.2 %fusion.1 = bf16[2048,19584]{1,0:T(8,128)(2,1)} fusion(bf16[2048,4]{1,0:T(8,128)(2,1)} %copy.76, bf16[2048,11264]{1,0:T(8,128)(2,1)} %convolution_convert_fusion, bf16[2048,2048]{1,0:T(8,128)(2,1)} %copy.77, bf16[2048,6144]{1,0:T(8,128)(2,1)} %convolution_convert_fusion.2), kind=kLoop, calls=%fused_computation.2 | loop fusion | flops 401080320 | bytes 159924224 | tf_op jit(solution)/shard_map/concatenate | solution.py:311
  963.0 5.4 multiply_add_fusion
  968.4 19.2 %convolution_add_fusion = f32[384,2048]{1,0:T(8,128)} fusion(f32[384,2048]{1,0:T(8,128)S(1)} %copy-done.7, bf16[384,5632]{1,0:T(8,128)(2,1)} %get-tuple-element.93, bf16[5632,2048]{1,0:T(8,128)(2,1)} %all-gather.11.cloned.1.call-done), kind=kOutput, calls=%fused_computation.63 | convolution fusion | flops 8859156480 | bytes 33685504 | tf_op jit(solution)/shard_map/dot_general | solution.py:24
  987.6 2.6 convert_element_type.111
  990.2 661.5 %reduce-scatter.3.cloned.1.call-done = bf16[64,19584]{1,0:T(8,128)(2,1)} async-done(((bf16[2048,19584]{1,0:T(8,128)(2,1)}), bf16[64,19584]{1,0:T(8,128)(2,1)}) %reduce-scatter.3.cloned.1.call-update) | async-done | bytes 2506768 | tf_op jit(solution)/shard_map/reduce_scatter | solution.py:181
  (103 shorter events, 30.8 us)
Async XLA Ops:
  7.2 164.1 %all-gather.5.cloned.1.call-start = ((), (), s32[]{:S(2)}) async-start(), calls=%async_computation.2 | async-start | bytes 26492928 | tf_op jit(solution)/shard_map/all_gather | solution.py:177
  10.1 4.1 copy-start.17
  10.1 6.6 copy-start
  10.1 244.2 %all-gather.7.cloned.1.call-start = ((), (), s32[]{:S(2)}) async-start(), calls=%async_computation.3 | async-start | bytes 8650752 | tf_op jit(solution)/shard_map/all_gather | solution.py:177
  10.9 497.1 %all-gather.9.cloned.1.call-start = ((), (), s32[]{:S(2)}) async-start(), calls=%async_computation.4 | async-start | bytes 47579136 | tf_op jit(solution)/shard_map/all_gather | solution.py:177
  13.6 640.0 %all-gather.11.cloned.1.call-start = ((), (), s32[]{:S(2)}) async-start(), calls=%async_computation.5 | async-start | bytes 23789568 | tf_op jit(solution)/shard_map/all_gather | solution.py:177
  14.2 973.4 %reduce-scatter.5.cloned.1.call-start = ((), (), s32[]{:S(2)}) async-start(), calls=%async_computation.7 | async-start | bytes 23789568 | tf_op jit(solution)/shard_map/reduce_scatter | solution.py:181
  14.3 5.7 collective-permute-start
  16.7 1.9 copy-start.4
  18.6 156.4 %copy-start.13 = (f32[384]{0:T(512)}, f32[384]{0:T(512)S(1)}, u32[]{:S(2)}) copy-start(f32[384]{0:T(512)S(1)} %rsqrt_bitcast_fusion) | copy-start | bytes 4612
  20.1 173.7 %copy-start.15 = (f32[384]{0:T(512)}, f32[384]{0:T(512)S(1)}, u32[]{:S(2)}) copy-start(f32[384]{0:T(512)S(1)} %fusion.62) | copy-start | bytes 4612
  175.1 18.8 %copy-start.11 = (f32[1,2048]{1,0:T(1,128)}, f32[1,2048]{1,0:T(1,128)S(1)}, u32[]{:S(2)}) copy-start(f32[1,2048]{1,0:T(1,128)S(1)} %get-tuple-element.108) | copy-start | bytes 24580
  175.4 18.4 %copy-start.8 = (bf16[384,2048]{1,0:T(8,128)(2,1)}, bf16[384,2048]{1,0:T(8,128)(2,1)S(1)}, u32[]{:S(2)}) copy-start(bf16[384,2048]{1,0:T(8,128)(2,1)S(1)} %multiply_convert_fusion.8) | copy-start | bytes 4718596
  230.4 0.6 copy-start.9
  245.9 0.8 copy-start.6
  696.7 955.0 %reduce-scatter.3.cloned.1.call-start = ((), (), s32[]{:S(2)}) async-start(), calls=%async_computation.6 | async-start | bytes 82722816 | tf_op jit(solution)/shard_map/reduce_scatter | solution.py:181
  737.1 9.9 copy-start.5
  752.1 37.2 %copy-start.10 = (bf16[1,1,3,2048]{3,2,1,0:T(4,128)(2,1)S(1)}, bf16[1,1,3,2048]{3,2,1,0:T(4,128)(2,1)}, u32[]{:S(2)}) copy-start(bf16[1,1,3,2048]{3,2,1,0:T(4,128)(2,1)} %copy-done.9) | copy-start | bytes 36868
  752.1 52.6 %copy-start.3 = (f32[3,128,2048]{2,1,0:T(8,128)S(1)}, f32[3,128,2048]{2,1,0:T(8,128)}, u32[]{:S(2)}) copy-start(f32[3,128,2048]{2,1,0:T(8,128)} %pad_maximum_fusion.3) | copy-start | bytes 9437188
  752.1 52.6 %copy-start.16 = (f32[384]{0:T(512)S(1)}, f32[384]{0:T(512)}, u32[]{:S(2)}) copy-start(f32[384]{0:T(512)} %copy-done.15) | copy-start | bytes 4612
  812.1 4.1 copy-start.1
  812.1 4.1 copy-start.12
  812.1 4.1 copy-start.14
  963.0 5.4 copy-start.7
  1651.7 2.9 copy-start.2
Sparse Core Ops, SparseCore 0:
  11.4 159.8 all-gather.4
  174.3 76.3 all-gather.6
  254.1 253.8 all-gather.8
  510.7 142.7 all-gather.10
  696.8 251.8 reduce-scatter.4
  963.1 688.5 reduce-scatter.2

commit v2 on v1

--- a/solution.py
+++ b/solution.py
@@ -1,3 +1,5 @@
+import functools
+
 import jax
 import jax.numpy as jnp
 from jax import lax
@@ -9,6 +11,8 @@
 ALL = ("dp", "seq")
 LANES = 128
 SUB = 8
+MESH = pl.DeviceIdType.MESH
+SLOTS = 2
 
 
 def silu_slope(values):
@@ -171,6 +175,334 @@
     for k in range(parts - 1, 0, -1):
         total = jnp.where(k > place, both[k, 0] * total + both[k, 1], total)
     return total
+
+
+def split_mesh(dp, seq):
+    side = max(d for d in range(1, dp + 1) if dp % d == 0 and d * d <= dp)
+    return dp // side, side, seq // 2
+
+
+def locate(dims):
+    Y, X, Z = dims
+    dp, seq = lax.axis_index("dp"), lax.axis_index("seq")
+    return lax.div(dp, X), lax.rem(dp, X), lax.div(seq, 2), lax.rem(seq, 2)
+
+
+def device(dims, y, x, z, c):
+    return (y * dims[1] + x, z * 2 + c)
+
+
+def hop(place, k, size):
+    return lax.rem(place + k, size)
+
+
+def greet(dims, here):
+    Y, X, Z = dims
+    y, x, z, c = here
+    barrier = pltpu.get_barrier_semaphore()
+    peers = [device(dims, y, x, z, 1 - c)]
+    peers += [device(dims, hop(y, k, Y), x, z, c) for k in range(1, Y)]
+    peers += [device(dims, y, hop(x, k, X), z, c) for k in range(1, X)]
+    peers += [device(dims, y, x, hop(z, k, Z), c) for k in range(1, Z)]
+    for peer in peers:
+        pl.semaphore_signal(barrier, inc=1, device_id=peer, device_id_type=MESH)
+    pl.semaphore_wait(barrier, len(peers))
+
+
+def scatter_kernel(dims, depth, wide, pairs, spans, has_vec, *refs):
+    Y, X, Z = dims
+    half = wide // 2
+    f32, low = jnp.float32, jnp.bfloat16
+    refs = list(refs)
+    take = lambda n: [refs.pop(0) for _ in range(n)]
+    lefts, rights = take(pairs), take(pairs)
+    vec = take(1)[0] if has_vec else None
+    outs = take(len(spans))
+    (part, core_in, one_a, one_b, in_a, in_b, two_a, two_b, far_a, far_b, three, line_in) = take(12)
+    (core_s, core_r, ya_s, ya_r, xb_s, xb_r, xa_s, xa_r, yb_s, yb_r, z_s, z_r) = take(12)
+    (core_f, ya_f, xb_f, xa_f, yb_f, z_f) = take(6)
+    here = locate(dims)
+    y, x, z, c = here
+    greet(dims, here)
+    total = spans[-1][2]
+
+    def send(src, dst, ss, rs, peer):
+        return pltpu.make_async_remote_copy(
+            src_ref=src, dst_ref=dst, send_sem=ss, recv_sem=rs, device_id=peer, device_id_type=MESH
+        )
+
+    def core_copies(t):
+        s = lax.rem(t, SLOTS)
+        return [
+            (
+                send(part.at[s, 1 - c], core_in.at[s], core_s.at[s], core_r.at[s],
+                     device(dims, y, x, z, 1 - c)),
+                core_f.at[0],
+                device(dims, y, x, z, 1 - c),
+            )
+        ]
+
+    def first_copies(t):
+        s = lax.rem(t, SLOTS)
+        out = []
+        for k in range(1, Y):
+            to, frm = hop(y, k, Y), hop(y, Y - k, Y)
+            out.append(
+                (
+                    send(one_a.at[s, to], in_a.at[s, k - 1], ya_s.at[s, k - 1], ya_r.at[s, k - 1],
+                         device(dims, to, x, z, c)),
+                    ya_f.at[k - 1],
+                    device(dims, frm, x, z, c),
+                )
+            )
+        for k in range(1, X):
+            to, frm = hop(x, k, X), hop(x, X - k, X)
+            out.append(
+                (
+                    send(one_b.at[s, to], in_b.at[s, k - 1], xb_s.at[s, k - 1], xb_r.at[s, k - 1],
+                         device(dims, y, to, z, c)),
+                    xb_f.at[k - 1],
+                    device(dims, y, frm, z, c),
+                )
+            )
+        return out
+
+    def second_copies(t):
+        s = lax.rem(t, SLOTS)
+        out = []
+        for k in range(1, X):
+            to, frm = hop(x, k, X), hop(x, X - k, X)
+            out.append(
+                (
+                    send(two_a.at[s, to], far_a.at[s, k - 1], xa_s.at[s, k - 1], xa_r.at[s, k - 1],
+                         device(dims, y, to, z, c)),
+                    xa_f.at[k - 1],
+                    device(dims, y, frm, z, c),
+                )
+            )
+        for k in range(1, Y):
+            to, frm = hop(y, k, Y), hop(y, Y - k, Y)
+            out.append(
+                (
+                    send(two_b.at[s, to], far_b.at[s, k - 1], yb_s.at[s, k - 1], yb_r.at[s, k - 1],
+                         device(dims, to, x, z, c)),
+                    yb_f.at[k - 1],
+                    device(dims, frm, x, z, c),
+                )
+            )
+        return out
+
+    def line_copies(t):
+        s = lax.rem(t, SLOTS)
+        out = []
+        for k in range(1, Z):
+            to, frm = hop(z, k, Z), hop(z, Z - k, Z)
+            out.append(
+                (
+                    send(three.at[s, to], line_in.at[s, k - 1], z_s.at[s, k - 1], z_r.at[s, k - 1],
+                         device(dims, y, x, to, c)),
+                    z_f.at[k - 1],
+                    device(dims, y, x, frm, c),
+                )
+            )
+        return out
+
+    def begin(copies, t):
+        for copy, free, _ in copies:
+
+            @pl.when(t >= SLOTS)
+            def _():
+                pl.semaphore_wait(free, 1)
+
+            copy.start()
+
+    def arrive(copies):
+        for copy, _, _ in copies:
+            copy.wait()
+
+    def release(copies, t):
+        for _, free, giver in copies:
+
+            @pl.when(t + SLOTS < total)
+            def _():
+                pl.semaphore_signal(free, inc=1, device_id=giver, device_id_type=MESH)
+
+    def produce(t):
+        s = lax.rem(t, SLOTS)
+        for pair in range(pairs):
+            low_t, high_t = rights_span[pair]
+
+            @pl.when(jnp.logical_and(t >= low_t, t < high_t))
+            def _():
+                columns = pl.ds(pl.multiple_of((t - low_t) * wide, wide), wide)
+
+                def block(i, _):
+                    rows = Z * 2 * depth
+                    first = pl.multiple_of(i * rows, rows)
+                    value = jnp.dot(
+                        lefts[pair][pl.ds(first, rows), :],
+                        rights[pair][:, columns],
+                        preferred_element_type=f32,
+                    ).astype(low)
+                    value = value.reshape(Z, 2, depth, wide)
+                    for core in range(2):
+                        part[s, core, lax.div(i, X), lax.rem(i, X)] = value[:, core]
+                    return 0
+
+                lax.fori_loop(0, Y * X, block, 0)
+
+        if has_vec:
+
+            @pl.when(t == total - 1)
+            def _():
+                def block(i, _):
+                    rows = Z * 2 * depth
+                    first = pl.multiple_of(i * rows, rows)
+                    value = vec[pl.ds(first, rows), :].reshape(Z, 2, depth, vec.shape[1])
+                    for core in range(2):
+                        part[s, core, lax.div(i, X), lax.rem(i, X), :, :, : vec.shape[1]] = value[
+                            :, core
+                        ]
+                    return 0
+
+                lax.fori_loop(0, Y * X, block, 0)
+
+    rights_span = []
+    start = 0
+    for pair in range(pairs):
+        count = rights[pair].shape[1] // wide
+        rights_span.append((start, start + count))
+        start += count
+
+    def step(t, _):
+        @pl.when(t < total)
+        def _():
+            produce(t)
+            begin(core_copies(t), t)
+
+        u = t - 1
+
+        @pl.when(jnp.logical_and(u >= 0, u < total))
+        def _():
+            s = lax.rem(u, SLOTS)
+            copies = core_copies(u)
+            arrive(copies)
+
+            def block(i, _):
+                i, j = lax.div(i, X), lax.rem(i, X)
+                value = part[s, c, i, j].astype(f32) + core_in[s, i, j].astype(f32)
+                value = value.astype(low)
+                one_a[s, i, j] = value[:, :, :half]
+                one_b[s, j, i] = value[:, :, half:]
+                return 0
+
+            lax.fori_loop(0, Y * X, block, 0)
+            release(copies, u)
+            begin(first_copies(u), u)
+
+        v = t - 2
+
+        @pl.when(jnp.logical_and(v >= 0, v < total))
+        def _():
+            s = lax.rem(v, SLOTS)
+            copies = first_copies(v)
+            arrive(copies)
+            value = one_a[s, y].astype(f32)
+            for k in range(Y - 1):
+                value = value + in_a[s, k].astype(f32)
+            two_a[s] = value.astype(low)
+            value = one_b[s, x].astype(f32)
+            for k in range(X - 1):
+                value = value + in_b[s, k].astype(f32)
+            two_b[s] = value.astype(low)
+            release(copies, v)
+            begin(second_copies(v), v)
+
+        w = t - 3
+
+        @pl.when(jnp.logical_and(w >= 0, w < total))
+        def _():
+            s = lax.rem(w, SLOTS)
+            copies = second_copies(w)
+            arrive(copies)
+            value = two_a[s, x].astype(f32)
+            for k in range(X - 1):
+                value = value + far_a[s, k].astype(f32)
+            three[s, :, :, :half] = value.astype(low)
+            value = two_b[s, y].astype(f32)
+            for k in range(Y - 1):
+                value = value + far_b[s, k].astype(f32)
+            three[s, :, :, half:] = value.astype(low)
+            release(copies, w)
+            begin(line_copies(w), w)
+
+        q = t - 4
+
+        @pl.when(q >= 0)
+        def _():
+            s = lax.rem(q, SLOTS)
+            copies = line_copies(q)
+            arrive(copies)
+            value = three[s, z].astype(f32)
+            for k in range(Z - 1):
+                value = value + line_in[s, k].astype(f32)
+            release(copies, q)
+            for index, (_, low_t, high_t) in enumerate(spans):
+
+                @pl.when(jnp.logical_and(q >= low_t, q < high_t))
+                def _():
+                    outs[index][:, pl.ds(pl.multiple_of((q - low_t) * wide, wide), wide)] = value
+
+        return 0
+
+    lax.fori_loop(0, total + 4, step, 0)
+
+
+def scatter_call(dims, depth, wide, pairs, widths, vec, collective_id):
+    Y, X, Z = dims
+    half = wide // 2
+    low = jnp.bfloat16
+    widths = list(widths)
+    if vec is not None:
+        widths.append(wide)
+    spans, start = [], 0
+    for n in widths:
+        spans.append((n, start, start + n // wide))
+        start += n // wide
+    operands = [a for a, _ in pairs] + [b for _, b in pairs] + ([vec] if vec is not None else [])
+    vmem = lambda *shape: pltpu.VMEM((SLOTS,) + shape, low)
+    dma = lambda *shape: pltpu.SemaphoreType.DMA((SLOTS,) + shape)
+    reg = lambda n: pltpu.SemaphoreType.REGULAR((n,))
+    y1, x1, z1 = max(Y - 1, 1), max(X - 1, 1), max(Z - 1, 1)
+    scratch = [
+        vmem(2, Y, X, Z, depth, wide),
+        vmem(Y, X, Z, depth, wide),
+        vmem(Y, X, Z, depth, half),
+        vmem(X, Y, Z, depth, half),
+        vmem(y1, X, Z, depth, half),
+        vmem(x1, Y, Z, depth, half),
+        vmem(X, Z, depth, half),
+        vmem(Y, Z, depth, half),
+        vmem(x1, Z, depth, half),
+        vmem(y1, Z, depth, half),
+        vmem(Z, depth, wide),
+        vmem(z1, depth, wide),
+    ]
+    scratch += [dma(), dma()]
+    scratch += [dma(y1), dma(y1), dma(x1), dma(x1), dma(x1), dma(x1), dma(y1), dma(y1), dma(z1), dma(z1)]
+    scratch += [reg(1), reg(y1), reg(x1), reg(x1), reg(y1), reg(z1)]
+    return pl.pallas_call(
+        functools.partial(
+            scatter_kernel, dims, depth, wide, len(pairs), spans, vec is not None
+        ),
+        out_shape=[jax.ShapeDtypeStruct((depth, n), jnp.float32) for n in widths],
+        in_specs=[pl.BlockSpec(memory_space=pltpu.VMEM)] * len(operands),
+        out_specs=[pl.BlockSpec(memory_space=pltpu.VMEM)] * len(widths),
+        scratch_shapes=scratch,
+        compiler_params=pltpu.CompilerParams(
+            collective_id=collective_id, has_side_effects=True, vmem_limit_bytes=60 * 2**20
+        ),
+    )(*operands)
 
 
 def gather_all(shard):
@@ -307,32 +639,60 @@
 
     low = jnp.bfloat16
     vector_sums = jnp.stack([gain_one, floor_sum, gain_out, gain_two], axis=1)
-    terms = scatter_all(
-        jnp.concatenate(
-            [
-                contract_rows(normed_one, grad_pre[:, : 3 * width]).astype(low),
-                contract_rows(mixed, grad_mixer).astype(low),
-                contract_rows(normed_two, grad_up).astype(low),
-                jnp.pad(vector_sums, ((0, 0), (0, LANES - 4))).astype(low),
-            ],
-            axis=1,
+    vector_sums = jnp.pad(vector_sums, ((0, 0), (0, LANES - 4))).astype(low)
+    depth, deep = output_proj.shape[0], down_proj.shape[0]
+    wide, narrow = 512, 256
+    own_kernel = (
+        depth % 16 == 0
+        and deep % 16 == 0
+        and parts % 2 == 0
+        and width % wide == 0
+        and hidden % wide == 0
+    )
+    if own_kernel:
+        dims = split_mesh(lax.axis_size("dp"), parts)
+        *grads, vector_terms = scatter_call(
+            dims,
+            depth,
+            wide,
+            [(normed_one.T, grad_pre), (mixed.T, grad_mixer), (normed_two.T, grad_up)],
+            [width] * 4 + [hidden] * 2,
+            vector_sums,
+            1,
         )
-    ).astype(jnp.float32)
-    down_grad = scatter_all(contract_rows(activated, grad_dense).astype(low)).astype(jnp.float32)
-    base = 4 * width + 2 * hidden
+        (down_grad,) = scatter_call(
+            dims, deep, narrow, [(activated.T, grad_dense)], [width], None, 2
+        )
+    else:
+        terms = scatter_all(
+            jnp.concatenate(
+                [
+                    contract_rows(normed_one, grad_pre[:, : 3 * width]).astype(low),
+                    contract_rows(mixed, grad_mixer).astype(low),
+                    contract_rows(normed_two, grad_up).astype(low),
+                    vector_sums,
+                ],
+                axis=1,
+            )
+        ).astype(jnp.float32)
+        marks = [width, 2 * width, 3 * width, 4 * width]
+        marks += [4 * width + hidden, 4 * width + 2 * hidden]
+        *grads, vector_terms = jnp.split(terms, marks, axis=1)
+        down_grad = scatter_all(contract_rows(activated, grad_dense).astype(low))
+        down_grad = down_grad.astype(jnp.float32)
     return (
         block_out,
         input_grad,
-        terms[:, base],
-        terms[:, :width],
-        terms[:, width : 2 * width],
-        terms[:, 2 * width : 3 * width],
-        terms[:, base + 1],
-        terms[:, base + 2],
-        terms[:, 3 * width : 4 * width],
-        terms[:, base + 3],
-        terms[:, 4 * width : 4 * width + hidden],
-        terms[:, 4 * width + hidden : base],
+        vector_terms[:, 0],
+        grads[0],
+        grads[1],
+        grads[2],
+        vector_terms[:, 1],
+        vector_terms[:, 2],
+        grads[3],
+        vector_terms[:, 3],
+        grads[4],
+        grads[5],
         down_grad,
     )
 

time: 1670 us -> 1370 us (0.82)
  waiting for transfers between devices: 1170 us -> 502 us
  Pallas kernels: 70.3 us -> 545 us
  matrix products: 239 us -> 154 us
  other arithmetic: 107 us -> 72.5 us
  local copies, waits for them, and re-layouts: 27.2 us -> 44.2 us
    reduce_scatter x2 -> x0, waiting for transfers between devices: 662 us -> none  [scatter_all(): return lax.psum_scatter(whole, ALL, scatter_dimension=0, tiled=True)]
    pallas_call x0 -> x2, Pallas kernels: none -> 475 us  [scatter_call(): pl.pallas_call(functools.partial(scatter_kernel, dims, depth, wide, len(p...]
    dot_general x4 -> x0, matrix products: 81.5 us -> none  [contract_rows(): lax.dot_general(left, right, (((0,), (0,)), ((), ())), preferred_element_...]
    concatenate x1 -> x2, other arithmetic: 52.2 us -> 21.7 us  [the longest x1 19.1 us: shards(): jnp.concatenate([(grad_act * up_two * silu_slope(up_one)).astype(jnp.bflo...]
  transfers between devices with their start and end apart: 7 -> 5, of which waited for: 4 -> 3; matrix products, arithmetic and copies ran while one was open for 19% -> 6% of each run, Pallas kernels for 4% -> 2%
where the time goes in v2:
time: 1370 us; the launch traced here: 1360 us
  Pallas kernels  545 us (40%)
  waiting for transfers between devices  502 us (37%)
  matrix products  154 us (11%)
  other arithmetic  72.5 us (5%)
  local copies, waits for them, and re-layouts  44.2 us (3%)
  blocking collectives  28.8 us (2%)
  between operations  14.4 us (1%)
    all_gather x4, waiting for transfers between devices, gather_all(): return lax.all_gather(shard, ALL, axis=0, tiled=True)  501 us
    pallas_call x2, Pallas kernels, scatter_call(): pl.pallas_call(functools.partial(scatter_kernel, dims, depth, wide, len(p...  475 us
    dot_general x4, matrix products, contract_last(): lax.dot_general(left, right, (((1,), (1,)), ((), ())), preferred_element_...  78.8 us
    dot_general x4, matrix products, dot(): return jnp.dot(left, right, preferred_element_type=jnp.float32)  75.4 us
    pallas_call x1, Pallas kernels, backward_scan(): pl.pallas_call(lambda *refs: backward_scan_kernel(span_len, *refs), grid=...  36.2 us
    pallas_call x1, Pallas kernels, forward_scan(): pl.pallas_call(lambda *refs: forward_scan_kernel(span_len, *refs), grid=(...  34.1 us
  transfers between devices with their start and end apart: 5, of which 3 were waited for; matrix products, arithmetic and copies ran while one was open for 6% of the time, Pallas kernels for 2%

profile of v2, /device:TPU:0, one launch (start us, length us, event | category | flops | bytes accessed | tf_op | source)
XLA Modules:
  0.0 1364.3 jit_solution(11616724886125699487)
XLA Ops:
  10.9 2.7 pad_maximum_fusion.2
  14.3 2.3 collective-permute-start
  20.0 151.3 %all-gather.5.cloned.1.call-done = bf16[2048,6272]{1,0:T(8,128)(2,1)} async-done(((bf16[64,6272]{1,0:T(8,128)(2,1)}), bf16[2048,6272]{1,0:T(8,128)(2,1)}) %all-gather.5.cloned.1.call-update) | async-done | bytes 25690128 | tf_op jit(solution)/shard_map/all_gather | solution.py:509
  176.5 2.7 copy.102.refs_0_
  179.2 18.0 %fusion.54.refs_0_.refs_1_ = f32[384,6272]{1,0:T(8,128)} fusion(bf16[384,2048]{1,0:T(8,128)(2,1)S(1)} %copy-done.10, bf16[2048,6272]{1,0:T(8,128)(2,1)} %all-gather.5.cloned.1.call-done), kind=kOutput, calls=%fused_computation.163 | convolution fusion | flops 9865003008 | bytes 36896768 | tf_op jit(solution)/shard_map/dot_general | solution.py:28
  198.0 34.1 %shard_map.237 = (f32[384,2048]{1,0:T(8,128)}, f32[384,2048]{1,0:T(8,128)}) custom-call(f32[384,6272]{1,0:T(8,128)} %fusion.54.refs_0_.refs_1_, f32[384,6272]{1,0:T(8,128)} %fusion.54.refs_0_.refs_1_, f32[1,2048]{1,0:T(1,128)} %get-tuple-element.118.refs_2_, f32[384,128]{1,0:T(8,128)} %broadcast_in_dim.9.refs_3_), custom_call_target="tpu_custom_call" | custom-call | tf_op jit(solution)/shard_map/pallas_call | solution.py:127
  234.7 14.7 %all_gather.21 = bf16[8,2,3,2048]{3,1,2,0:T(2,128)(2,1)S(1)} all-gather(bf16[1,2,3,2048]{3,1,2,0:T(2,128)(2,1)S(1)} %copy.89), channel_id=1, replica_groups=mesh['dp'=4,'seq'=8] {'seq'}, dimensions={0}, use_global_device_ids=true | all-gather | bytes 221184 | tf_op jit(solution)/shard_map/all_gather | solution.py:164
  250.4 3.4 multiply_reduce_fusion.7
  253.7 4.1 multiply_convert_fusion.7
  260.0 9.8 multiply_reduce_fusion.6
  272.9 235.7 %all-gather.9.cloned.1.call-done = bf16[2048,11264]{1,0:T(8,128)(2,1)} async-done(((bf16[64,11264]{1,0:T(8,128)(2,1)}), bf16[2048,11264]{1,0:T(8,128)(2,1)}) %all-gather.9.cloned.1.call-update) | async-done | bytes 46137360 | tf_op jit(solution)/shard_map/all_gather | solution.py:509
  508.7 31.3 %fusion.46 = f32[384,11264]{0,1:T(8,128)} fusion(bf16[2048,11264]{1,0:T(8,128)(2,1)} %all-gather.9.cloned.1.call-done, f32[384,2048]{1,0:T(8,128)S(1)} %get-tuple-element.121, f32[2048]{0:T(1024)S(1)} %bitcast.439, f32[384]{0:T(512)S(1)} %add_rsqrt_fusion), kind=kOutput, calls=%fused_computation.158 | convolution fusion | flops 17719099392 | bytes 66594304 | tf_op jit(solution)/shard_map/dot_general | solution.py:28
  540.0 114.2 %all-gather.11.cloned.1.call-done = bf16[5632,2048]{1,0:T(8,128)(2,1)} async-done(((bf16[176,2048]{1,0:T(8,128)(2,1)}), bf16[5632,2048]{1,0:T(8,128)(2,1)}) %all-gather.11.cloned.1.call-update) | async-done | bytes 23068688 | tf_op jit(solution)/shard_map/all_gather | solution.py:509
  654.2 22.4 %multiply_convert_fusion.1 = (bf16[384,5632]{0,1:T(8,128)(2,1)S(1)}, bf16[384,5632]{0,1:T(8,128)(2,1)S(1)}, bf16[384,5632]{0,1:T(8,128)(2,1)}) fusion(f32[384,11264]{0,1:T(8,128)} %fusion.46, bf16[384,2048]{1,0:T(8,128)(2,1)} %bitcast_convert_fusion.refs_1_, bf16[5632,2048]{1,0:T(8,128)(2,1)} %all-gather.11.cloned.1.call-done), kind=kOutput, calls=%fused_computation.2 | convolution fusion | flops 8890810368 | bytes 54919168 | tf_op jit(solution)/shard_map/dot_general | solution.py:32
  680.0 19.1 %pad_maximum_fusion = bf16[384,11264]{0,1:T(8,128)(2,1)} fusion(bf16[384,5632]{0,1:T(8,128)(2,1)S(1)} %get-tuple-element.108, bf16[384,5632]{0,1:T(8,128)(2,1)S(1)} %get-tuple-element.107), kind=kLoop, calls=%fused_computation | loop fusion | flops 17301504 | bytes 17301504 | tf_op jit(solution)/shard_map/concatenate | solution.py:592
  699.2 11.9 copy.105.refs_5_
  711.1 119.4 %shard_map.240 = f32[176,2048]{1,0:T(8,128)} custom-call(bf16[5632,384]{1,0:T(8,128)(2,1)} %bitcast.425, bf16[384,2048]{1,0:T(8,128)(2,1)} %bitcast_convert_fusion.refs_1_), custom_call_target="tpu_custom_call" | custom-call | tf_op jit(solution)/shard_map/pallas_call | solution.py:494
  830.4 26.8 %fusion.47 = f32[384,2048]{1,0:T(8,128)} fusion(bf16[2048,11264]{1,0:T(8,128)(2,1)} %all-gather.9.cloned.1.call-done, bf16[384,5632]{0,1:T(8,128)(2,1)} %copy-done.16, bf16[384,5632]{0,1:T(8,128)(2,1)} %copy-done.15), kind=kOutput, calls=%fused_computation.159 | convolution fusion | flops 17734041600 | bytes 57933824 | tf_op jit(solution)/shard_map/dot_general | solution.py:32
  857.2 4.1 multiply_reduce_fusion
  861.3 2.5 fusion.52
  863.9 10.7 multiply_reduce_fusion.1
  874.6 2.6 copy.104.refs_2_
  877.2 6.7 subtract_multiply_fusion
  883.9 36.2 %shard_map.238 = (f32[384,2048]{1,0:T(8,128)}, f32[384,2048]{1,0:T(8,128)}, f32[3,2048]{1,0:T(4,128)}) custom-call(f32[384,2048]{1,0:T(8,128)} %get-tuple-element.111.refs_0_, f32[384,6272]{1,0:T(8,128)} %fusion.54.refs_0_.refs_1_, f32[1,2048]{1,0:T(1,128)} %get-tuple-element.118.refs_2_, f32[384,128]{1,0:T(8,128)} %broadcast_in_dim.9.refs_3_), custom_call_target="tpu_custom_call" | custom-call | tf_op jit(solution)/shard_map/pallas_call | solution.py:147
  921.0 14.1 %all_gather.25 = bf16[8,2,3,2048]{3,1,2,0:T(2,128)(2,1)S(1)} all-gather(bf16[1,2,3,2048]{3,1,2,0:T(2,128)(2,1)S(1)} %copy.96), channel_id=1, replica_groups=mesh['dp'=4,'seq'=8] {'seq'}, dimensions={0}, use_global_device_ids=true | all-gather | bytes 221184 | tf_op jit(solution)/shard_map/all_gather | solution.py:173
  935.3 7.0 fusion.49
  942.3 3.3 multiply_convert_fusion.4
  946.9 2.6 maximum_maximum_fusion.refs_3_
  949.5 18.8 %multiply_reduce_fusion.2 = (bf16[2048]{0:T(1024)(128)(2,1)S(1)}, f32[384]{0:T(512)S(1)}, f32[384,2048]{1,0:T(8,128)}) fusion(f32[3,1,128,2048]{3,2,1,0:T(8,128)} %param.14, f32[384]{0:T(512)S(1)} %copy-done.31, f32[2048]{0:T(1024)S(1)} %bitcast.443, bf16[2048,6272]{1,0:T(8,128)(2,1)} %all-gather.5.cloned.1.call-done, ...), kind=kOutput, calls=%fused_computation.24 | convolution fusion | flops 9888987136 | bytes 36728064 | tf_op jit(solution)/shard_map/dot_general | solution.py:32
  971.3 355.7 %shard_map.239 = (f32[64,2048]{1,0:T(8,128)}, f32[64,2048]{1,0:T(8,128)}, f32[64,2048]{1,0:T(8,128)}, f32[64,2048]{1,0:T(8,128)}, f32[64,5632]{1,0:T(8,128)}, /*index=5*/f32[64,5632]{1,0:T(8,128)}, f32[64,512]{1,0:T(8,128)}) custom-call(bf16[2048,384]{1,0:T(8,128)(2,1)} %copy.102.refs_0_, bf16[2048,384]{1,0:T(8,128)(2,1)} %copy.103.refs_1_, ...), custom_call_target="tpu_custom_call" | custom-call | tf_op jit(solution)/shard_map/pallas_call | solution.py:494
  1328.7 6.2 multiply_add_fusion
  1334.9 16.2 %convolution_add_fusion = f32[384,2048]{1,0:T(8,128)} fusion(f32[384,2048]{1,0:T(8,128)S(1)} %get-tuple-element.121, bf16[384,5632]{0,1:T(8,128)(2,1)} %get-tuple-element.109, bf16[5632,2048]{1,0:T(8,128)(2,1)} %all-gather.11.cloned.1.call-done), kind=kOutput, calls=%fused_computation.44 | convolution fusion | flops 8859156480 | bytes 33685504 | tf_op jit(solution)/shard_map/dot_general | solution.py:28
  (138 shorter events, 39.4 us)
Async XLA Ops:
  7.2 164.1 %all-gather.5.cloned.1.call-start = ((), (), s32[]{:S(2)}) async-start(), calls=%async_computation | async-start | bytes 26492928 | tf_op jit(solution)/shard_map/all_gather | solution.py:509
  10.1 4.1 copy-start.34
  10.1 7.2 copy-start.2
  10.1 249.8 %all-gather.7.cloned.1.call-start = ((), (), s32[]{:S(2)}) async-start(), calls=%async_computation.1 | async-start | bytes 8650752 | tf_op jit(solution)/shard_map/all_gather | solution.py:509
  10.9 497.8 %all-gather.9.cloned.1.call-start = ((), (), s32[]{:S(2)}) async-start(), calls=%async_computation.2 | async-start | bytes 47579136 | tf_op jit(solution)/shard_map/all_gather | solution.py:509
  13.6 640.6 %all-gather.11.cloned.1.call-start = ((), (), s32[]{:S(2)}) async-start(), calls=%async_computation.3 | async-start | bytes 23789568 | tf_op jit(solution)/shard_map/all_gather | solution.py:509
  14.3 5.7 collective-permute-start
  18.6 156.5 %copy-start.30 = (f32[384]{0:T(512)}, f32[384]{0:T(512)S(1)}, u32[]{:S(2)}) copy-start(f32[384]{0:T(512)S(1)} %rsqrt_bitcast_fusion) | copy-start | bytes 4612
  20.0 177.2 %copy-start.32 = (f32[384]{0:T(512)}, f32[384]{0:T(512)S(1)}, u32[]{:S(2)}) copy-start(f32[384]{0:T(512)S(1)} %fusion.43) | copy-start | bytes 4612
  175.1 4.2 copy-start.27
  176.5 2.7 copy-start.10
  253.7 4.1 copy-start
  260.0 9.8 copy-start.18
  260.0 10.0 copy-start.3
  260.0 10.0 copy-start.4
  676.7 3.4 copy-start.16
  857.2 4.1 copy-start.6
  857.2 4.1 copy-start.7
  861.3 2.5 copy-start.1
  863.9 10.7 copy-start.8
  883.9 37.0 %copy-start.26 = (bf16[1,1,3,2048]{3,2,1,0:T(4,128)(2,1)S(1)}, bf16[1,1,3,2048]{3,2,1,0:T(4,128)(2,1)}, u32[]{:S(2)}) copy-start(bf16[1,1,3,2048]{3,2,1,0:T(4,128)(2,1)} %copy-done.25) | copy-start | bytes 36868
  883.9 51.4 %copy-start.33 = (f32[384]{0:T(512)S(1)}, f32[384]{0:T(512)}, u32[]{:S(2)}) copy-start(f32[384]{0:T(512)} %copy-done.32) | copy-start | bytes 4612
  942.3 3.4 copy-start.12
  942.3 4.5 copy-start.11
  942.3 4.5 copy-start.29
  946.8 2.6 copy-start.28
  946.9 2.6 copy-start.31
  1334.9 16.2 %copy-start.24 = (f32[64,2048]{1,0:T(8,128)S(1)}, f32[64,2048]{1,0:T(8,128)}, u32[]{:S(2)}) copy-start(f32[64,2048]{1,0:T(8,128)} %get-tuple-element.142) | copy-start | bytes 1572868
  1334.9 17.0 %copy-start.23 = (f32[64,2048]{1,0:T(8,128)S(1)}, f32[64,2048]{1,0:T(8,128)}, u32[]{:S(2)}) copy-start(f32[64,2048]{1,0:T(8,128)} %get-tuple-element.143) | copy-start | bytes 1572868
  1334.9 17.8 %copy-start.22 = (f32[64,2048]{1,0:T(8,128)S(1)}, f32[64,2048]{1,0:T(8,128)}, u32[]{:S(2)}) copy-start(f32[64,2048]{1,0:T(8,128)} %get-tuple-element.144) | copy-start | bytes 1572868
  1351.1 3.2 copy-start.20
  1351.9 3.5 copy-start.19
  (8 other events, 13.3 us)
Sparse Core Ops, SparseCore 0:
  11.4 159.8 all-gather.4
  174.3 76.9 all-gather.6
  254.7 253.9 all-gather.8
  511.4 142.7 all-gather.10

commit v3 on v2

--- a/solution.py
+++ b/solution.py
@@ -13,6 +13,8 @@
 SUB = 8
 MESH = pl.DeviceIdType.MESH
 SLOTS = 2
+AHEAD = 12
+EXTRA = 256
 
 
 def silu_slope(values):
@@ -58,9 +60,10 @@
     width = pre_input.shape[1]
     groups = pre_input.shape[0] // span_len
 
-    def group(g, _):
-        def tile(i, carry):
-            prod_in, state_in = carry
+    def tile(i, carries):
+        out = []
+        for g in range(groups):
+            prod_in, state_in = carries[g]
             rows = pl.ds(pl.multiple_of(g * span_len + i * SUB, SUB), SUB)
             value = pre_input[rows, :]
             leak = scale * jax.nn.sigmoid(-pre_forget[rows, :])
@@ -73,14 +76,11 @@
             decay = decay * prod_in
             products[rows, :] = decay
             partial[rows, :] = state
-            return decay[SUB - 1 :, :], state[SUB - 1 :, :]
-
-        lax.fori_loop(
-            0, tiles, tile, (jnp.ones((1, width), jnp.float32), jnp.zeros((1, width), jnp.float32))
-        )
-        return 0
-
-    lax.fori_loop(0, groups, group, 0)
+            out.append((decay[SUB - 1 :, :], state[SUB - 1 :, :]))
+        return tuple(out)
+
+    start = (jnp.ones((1, width), jnp.float32), jnp.zeros((1, width), jnp.float32))
+    lax.fori_loop(0, tiles, tile, (start,) * groups)
 
 
 def backward_scan_kernel(span_len, grad_states, pre_forget, floor, link, local, carry_mult, head):
@@ -89,10 +89,11 @@
     width = grad_states.shape[1]
     groups = grad_states.shape[0] // span_len
 
-    def group(g, _):
-        def tile(k, carry):
-            prod_in, pass_in = carry
-            i = tiles - 1 - k
+    def tile(k, carries):
+        i = tiles - 1 - k
+        out = []
+        for g in range(groups):
+            prod_in, pass_in = carries[g]
             rows = pl.ds(pl.multiple_of(g * span_len + i * SUB, SUB), SUB)
             upstream = grad_states[rows, :]
             decay = (1.0 - scale * jax.nn.sigmoid(-pre_forget[rows, :])) * link[rows, :1]
@@ -104,19 +105,17 @@
             decay = decay * prod_in
             local[rows, :] = upstream + shift_up(passed, 1, pass_in)
             carry_mult[rows, :] = shift_up(decay, 1, prod_in)
-            return decay[:1, :], passed[:1, :]
-
-        prod_out, pass_out = lax.fori_loop(
-            0, tiles, tile, (jnp.ones((1, width), jnp.float32), jnp.zeros((1, width), jnp.float32))
-        )
-        head[pl.ds(g, 1), :] = pass_out
-        return 0
-
-    lax.fori_loop(0, groups, group, 0)
+            out.append((decay[:1, :], passed[:1, :]))
+        return tuple(out)
+
+    start = (jnp.ones((1, width), jnp.float32), jnp.zeros((1, width), jnp.float32))
+    ends = lax.fori_loop(0, tiles, tile, (start,) * groups)
+    for g in range(groups):
+        head[g : g + 1, :] = ends[g][1]
 
 
 def scan_block(width):
-    return 256 if width % 256 == 0 else width
+    return 512 if width % 512 == 0 else width
 
 
 def forward_scan(pre_all, floor, link, span_len, width):
@@ -159,21 +158,23 @@
     )(grad_states, pre_all, floor, link)
 
 
-def entering_forward(mult, value):
+def exchange(value):
+    return lax.all_gather(value.astype(jnp.bfloat16), "seq").astype(jnp.float32)
+
+
+def entering_forward(mults, values):
     parts, place = lax.axis_size("seq"), lax.axis_index("seq")
-    both = lax.all_gather(jnp.stack([mult, value]).astype(jnp.bfloat16), "seq").astype(jnp.float32)
-    total = jnp.zeros_like(value)
+    total = jnp.zeros_like(values[0])
     for k in range(parts - 1):
-        total = jnp.where(k < place, both[k, 0] * total + both[k, 1], total)
+        total = jnp.where(k < place, mults[k] * total + values[k], total)
     return total
 
 
-def entering_backward(mult, value):
+def entering_backward(mults, values):
     parts, place = lax.axis_size("seq"), lax.axis_index("seq")
-    both = lax.all_gather(jnp.stack([mult, value]).astype(jnp.bfloat16), "seq").astype(jnp.float32)
-    total = jnp.zeros_like(value)
+    total = jnp.zeros_like(values[0])
     for k in range(parts - 1, 0, -1):
-        total = jnp.where(k > place, both[k, 0] * total + both[k, 1], total)
+        total = jnp.where(k > place, mults[k] * total + values[k], total)
     return total
 
 
@@ -505,6 +506,187 @@
     )(*operands)
 
 
+def gather_kernel(dims, wides, *refs):
+    Y, X, Z = dims
+    refs = list(refs)
+    take = lambda n: [refs.pop(0) for _ in range(n)]
+    n = len(wides)
+    shards, wholes = take(n), take(n)
+    own_sem, zs, zr, first_s, first_r, next_s, next_r, cs, cr = take(9)
+    here = locate(dims)
+    y, x, z, c = here
+    greet(dims, here)
+
+    def send(src, dst, ss, rs, peer):
+        return pltpu.make_async_remote_copy(
+            src_ref=src, dst_ref=dst, send_sem=ss, recv_sem=rs, device_id=peer, device_id_type=MESH
+        )
+
+    def halves(i, t):
+        wide = wides[i]
+        h = wide // 2
+        a = pl.ds(pl.multiple_of(t * wide, h), h)
+        b = pl.ds(pl.multiple_of(t * wide + h, h), h)
+        return a, b
+
+    def to_x(k):
+        return device(dims, y, hop(x, k, X), z, c)
+
+    def to_y(k):
+        return device(dims, hop(y, k, Y), x, z, c)
+
+    def to_z(k):
+        return device(dims, y, x, hop(z, k, Z), c)
+
+    counts = [shards[i].shape[1] // wides[i] for i in range(n)]
+    bases = [sum(counts[:i]) for i in range(n)]
+
+    def route(sends, ss, rs, i, t):
+        s = lax.rem(bases[i] + t, AHEAD)
+        return [
+            send(src, dst, ss.at[s, n], rs.at[s, n], peer) for n, (src, dst, peer) in enumerate(sends)
+        ]
+
+    def line_copies(i, t):
+        shard, whole = shards[i], wholes[i]
+        columns = pl.ds(pl.multiple_of(t * wides[i], wides[i]), wides[i])
+        block = (shard.at[:, columns], whole.at[y, x, z, c, :, columns])
+        return route([block + (to_z(k),) for k in range(1, Z)], zs, zr, i, t)
+
+    def own_copies(i, t):
+        shard, whole = shards[i], wholes[i]
+        a, b = halves(i, t)
+        block_a = (shard.at[:, a], whole.at[y, x, z, c, :, a])
+        block_b = (shard.at[:, b], whole.at[y, x, z, c, :, b])
+        sends = [block_a + (to_x(k),) for k in range(1, X)]
+        sends += [block_b + (to_y(k),) for k in range(1, Y)]
+        return route(sends, zs, zr, i, t)
+
+    def first_copies(i, t):
+        whole = wholes[i]
+        a, b = halves(i, t)
+        block_a, block_b = whole.at[y, x, :, c, :, a], whole.at[y, x, :, c, :, b]
+        sends = [(block_a, block_a, to_x(k)) for k in range(1, X)]
+        sends += [(block_b, block_b, to_y(k)) for k in range(1, Y)]
+        return route(sends, first_s, first_r, i, t)
+
+    def middle_copies(i, t):
+        whole = wholes[i]
+        a, b = halves(i, t)
+        block_a, block_b = whole.at[y, :, z, c, :, a], whole.at[:, x, z, c, :, b]
+        sends = [(block_a, block_a, to_z(k)) for k in range(1, Z)]
+        sends += [(block_b, block_b, to_z(k)) for k in range(1, Z)]
+        return route(sends, first_s, first_r, i, t)
+
+    def second_copies(i, t):
+        whole = wholes[i]
+        a, b = halves(i, t)
+        block_a, block_b = whole.at[y, :, :, c, :, a], whole.at[:, x, :, c, :, b]
+        sends = [(block_a, block_a, to_y(k)) for k in range(1, Y)]
+        sends += [(block_b, block_b, to_x(k)) for k in range(1, X)]
+        return route(sends, next_s, next_r, i, t)
+
+    def core_copies(i, t):
+        whole = wholes[i]
+        wide = wides[i]
+        columns = pl.ds(pl.multiple_of(t * wide, wide), wide)
+        s = lax.rem(bases[i] + t, AHEAD)
+        block = whole.at[:, :, :, c, :, columns]
+        return [send(block, block, cs.at[s], cr.at[s], device(dims, y, x, z, 1 - c))]
+
+    own = [
+        pltpu.make_async_copy(shards[i], wholes[i].at[y, x, z, c], own_sem.at[i]) for i in range(n)
+    ]
+    for copy in own:
+        copy.start()
+
+    for i in range(n):
+        total = counts[i]
+
+        def either(t, inside, one, other, act):
+            late = lax.rem(bases[i] + t, 3) == 2
+
+            @pl.when(jnp.logical_and(inside, jnp.logical_not(late)))
+            def _():
+                for copy in one(i, t):
+                    act(copy)
+
+            @pl.when(jnp.logical_and(inside, late))
+            def _():
+                for copy in other(i, t):
+                    act(copy)
+
+        def start(copy):
+            copy.start()
+
+        def wait(copy):
+            copy.wait()
+
+        def step(t, _):
+            either(t, t < total, line_copies, own_copies, start)
+
+            u = t - 2
+            inside = jnp.logical_and(u >= 0, u < total)
+            either(u, inside, line_copies, own_copies, wait)
+            either(u, inside, first_copies, middle_copies, start)
+
+            v = t - 4
+            inside = jnp.logical_and(v >= 0, v < total)
+            either(v, inside, first_copies, middle_copies, wait)
+
+            @pl.when(inside)
+            def _():
+                for copy in second_copies(i, v):
+                    copy.start()
+
+            w = t - 6
+
+            @pl.when(jnp.logical_and(w >= 0, w < total))
+            def _():
+                for copy in second_copies(i, w):
+                    copy.wait()
+                for copy in core_copies(i, w):
+                    copy.start()
+
+            q = t - 8
+
+            @pl.when(q >= 0)
+            def _():
+                for copy in core_copies(i, q):
+                    copy.wait()
+
+            return 0
+
+        own[i].wait()
+        lax.fori_loop(0, total + 8, step, 0)
+
+
+def gather_call(dims, shards, wides, collective_id):
+    Y, X, Z = dims
+    n = len(shards)
+    dma = lambda *shape: pltpu.SemaphoreType.DMA(shape)
+    most = max(X + Y - 2, 2 * (Z - 1), 1)
+    wholes = pl.pallas_call(
+        functools.partial(gather_kernel, dims, wides),
+        out_shape=[
+            jax.ShapeDtypeStruct((Y, X, Z, 2) + shard.shape, shard.dtype) for shard in shards
+        ],
+        in_specs=[pl.BlockSpec(memory_space=pltpu.VMEM)] * n,
+        out_specs=[pl.BlockSpec(memory_space=pl.ANY)] * n,
+        scratch_shapes=[
+            dma(n),
+            dma(AHEAD, most), dma(AHEAD, most),
+            dma(AHEAD, most), dma(AHEAD, most),
+            dma(AHEAD, most), dma(AHEAD, most),
+            dma(AHEAD), dma(AHEAD),
+        ],
+        compiler_params=pltpu.CompilerParams(
+            collective_id=collective_id, has_side_effects=True
+        ),
+    )(*shards)
+    return [whole.reshape(-1, whole.shape[-1]) for whole in wholes]
+
+
 def gather_all(shard):
     return lax.all_gather(shard, ALL, axis=0, tiled=True)
 
@@ -537,14 +719,29 @@
     parts, place = lax.axis_size("seq"), lax.axis_index("seq")
 
     vectors = jnp.stack([mixer_gain, floor_log, output_gain, dense_gain], axis=1)
-    vectors = jnp.pad(vectors, ((0, 0), (0, LANES - 4)))
-    mix_full = gather_all(
-        jnp.concatenate([input_proj, forget_proj, gate_proj, vectors], axis=1)
+    vectors = jnp.pad(vectors, ((0, 0), (0, EXTRA - 4)))
+    depth, deep = output_proj.shape[0], down_proj.shape[0]
+    wide, narrow = 512, 256
+    own_kernel = (
+        depth % 16 == 0
+        and deep % 16 == 0
+        and parts % 2 == 0
+        and width % wide == 0
+        and hidden % wide == 0
     )
-    out_full = gather_all(output_proj)
-    up_full = gather_all(jnp.concatenate([up_first, up_second], axis=1))
+    dims = split_mesh(lax.axis_size("dp"), parts)
+    mix_shard = jnp.concatenate([input_proj, forget_proj, gate_proj, vectors], axis=1)
+    up_shard = jnp.concatenate([up_first, up_second], axis=1)
+    if own_kernel:
+        mix_full, out_full, up_full = gather_call(
+            dims, [mix_shard, output_proj, up_shard], [256] * 3, 0
+        )
+    else:
+        mix_full, out_full, up_full = [gather_all(a) for a in (mix_shard, output_proj, up_shard)]
+    gains = mix_full[:, 3 * width : 3 * width + 4].T
+    if own_kernel:
+        down_proj, gains = lax.optimization_barrier((down_proj, gains))
     down_full = gather_all(down_proj)
-    gains = mix_full[:, 3 * width : 3 * width + 4].T
     mixer_gain_all = gains[0:1].astype(jnp.float32)
     floor_all = gains[1:2].astype(jnp.float32)
     out_gain_all = gains[2:3].astype(jnp.float32)
@@ -567,10 +764,13 @@
 
     products, partial_state = forward_scan(pre_all, floor_all, link, span_len, width)
     products = products.reshape(groups, span_len, width)
-    span_mult = products[:, -1]
-    entering = entering_forward(
-        span_mult, partial_state.reshape(groups, span_len, width)[:, -1]
+    ends = exchange(
+        jnp.concatenate(
+            [products[:, -1], partial_state.reshape(groups, span_len, width)[:, -1]], axis=0
+        )
     )
+    span_mults = ends[:, :groups]
+    entering = entering_forward(span_mults, ends[:, groups:])
     states = products * entering[:, None, :] + partial_state.reshape(groups, span_len, width)
     states_flat = states.reshape(rows_all, width)
     state_scale = lax.rsqrt(jnp.mean(states_flat * states_flat, axis=1, keepdims=True) + norm_eps)
@@ -584,10 +784,11 @@
     up_both = dot(normed_two, up_full)
     up_one, up_two = up_both[:, :hidden], up_both[:, hidden:]
     activated = (jax.nn.silu(up_one) * up_two).astype(jnp.bfloat16)
-    block_out = (middle + dot(activated, down_full)).reshape(inputs.shape)
-
     grad_flat = cotangent.reshape(rows_all, width)
     grad_dense = grad_flat.astype(jnp.bfloat16)
+    down_part = contract_rows(activated, grad_dense).astype(jnp.bfloat16)
+    down_full, down_part = lax.optimization_barrier((down_full, down_part))
+    block_out = (middle + dot(activated, down_full)).reshape(inputs.shape)
     grad_act = contract_last(grad_dense, down_full)
     grad_up = jnp.concatenate(
         [
@@ -610,7 +811,7 @@
     local_grad, carry_mult, head_grad = backward_scan(
         grad_states, pre_all, floor_all, link, span_len, width
     )
-    arriving = entering_backward(span_mult, head_grad)
+    arriving = entering_backward(span_mults, exchange(head_grad))
     adjoint = (
         local_grad.reshape(groups, span_len, width)
         + carry_mult.reshape(groups, span_len, width) * arriving[:, None, :]
@@ -627,7 +828,7 @@
             grad_pre_input,
             grad_pre_forget,
             grad_pre_gate,
-            jnp.zeros((rows_all, LANES), jnp.bfloat16),
+            jnp.zeros((rows_all, EXTRA), jnp.bfloat16),
         ],
         axis=1,
     )
@@ -640,17 +841,7 @@
     low = jnp.bfloat16
     vector_sums = jnp.stack([gain_one, floor_sum, gain_out, gain_two], axis=1)
     vector_sums = jnp.pad(vector_sums, ((0, 0), (0, LANES - 4))).astype(low)
-    depth, deep = output_proj.shape[0], down_proj.shape[0]
-    wide, narrow = 512, 256
-    own_kernel = (
-        depth % 16 == 0
-        and deep % 16 == 0
-        and parts % 2 == 0
-        and width % wide == 0
-        and hidden % wide == 0
-    )
     if own_kernel:
-        dims = split_mesh(lax.axis_size("dp"), parts)
         *grads, vector_terms = scatter_call(
             dims,
             depth,
@@ -659,9 +850,6 @@
             [width] * 4 + [hidden] * 2,
             vector_sums,
             1,
-        )
-        (down_grad,) = scatter_call(
-            dims, deep, narrow, [(activated.T, grad_dense)], [width], None, 2
         )
     else:
         terms = scatter_all(
@@ -678,8 +866,7 @@
         marks = [width, 2 * width, 3 * width, 4 * width]
         marks += [4 * width + hidden, 4 * width + 2 * hidden]
         *grads, vector_terms = jnp.split(terms, marks, axis=1)
-        down_grad = scatter_all(contract_rows(activated, grad_dense).astype(low))
-        down_grad = down_grad.astype(jnp.float32)
+    down_grad = scatter_all(down_part).astype(jnp.float32)
     return (
         block_out,
         input_grad,

time: 1370 us -> 1110 us (0.81)
  waiting for transfers between devices: 502 us -> 22.8 us
  Pallas kernels: 545 us -> 752 us
    all_gather x4 -> x1, waiting for transfers between devices: 501 us -> 22.8 us  [gather_all(): return lax.all_gather(shard, ALL, axis=0, tiled=True)]
    pallas_call x0 -> x1, Pallas kernels: none -> 345 us  [gather_call(): pl.pallas_call(functools.partial(gather_kernel, dims, wides), out_shape=[...]
    pallas_call x2 -> x1, Pallas kernels: 475 us -> 386 us  [scatter_call(): pl.pallas_call(functools.partial(scatter_kernel, dims, depth, wide, len(p...]
    pallas_call x1, Pallas kernels: 36.2 us -> 11.4 us  [backward_scan(): pl.pallas_call(lambda *refs: backward_scan_kernel(span_len, *refs), grid=...]
    pallas_call x1, Pallas kernels: 34.1 us -> 9.98 us  [forward_scan(): pl.pallas_call(lambda *refs: forward_scan_kernel(span_len, *refs), grid=(...]
    dot_general x0 -> x1, matrix products: none -> 18.9 us  [contract_rows(): lax.dot_general(left, right, (((0,), (0,)), ((), ())), preferred_element_...]
  transfers between devices with their start and end apart: 5 -> 3, of which waited for: 3 -> 1; matrix products, arithmetic and copies ran while one was open for 6% -> 24% of each run, Pallas kernels for 2% -> 37%
where the time goes in v3:
time: 1110 us
  Pallas kernels  752 us (68%)
  matrix products  163 us (15%)
  other arithmetic  82.7 us (7%)
  local copies, waits for them, and re-layouts  34.9 us (3%)
  blocking collectives  33.7 us (3%)
  waiting for transfers between devices  22.8 us (2%)
  between operations  14.9 us (1%)
    pallas_call x1, Pallas kernels, scatter_call(): pl.pallas_call(functools.partial(scatter_kernel, dims, depth, wide, len(p...  386 us
    pallas_call x1, Pallas kernels, gather_call(): pl.pallas_call(functools.partial(gather_kernel, dims, wides), out_shape=[...  345 us
    dot_general x4, matrix products, contract_last(): lax.dot_general(left, right, (((1,), (1,)), ((), ())), preferred_element_...  75 us
    dot_general x4, matrix products, dot(): return jnp.dot(left, right, preferred_element_type=jnp.float32)  68.7 us
    all_gather x2, blocking collectives, exchange(): return lax.all_gather(value.astype(jnp.bfloat16), 'seq').astype(jnp.float32)  33.7 us
    all_gather x1, waiting for transfers between devices, gather_all(): return lax.all_gather(shard, ALL, axis=0, tiled=True)  22.8 us
  transfers between devices with their start and end apart: 3, of which 1 were waited for; matrix products, arithmetic and copies ran while one was open for 24% of the time, Pallas kernels for 37%

profile of v3, /device:TPU:0, one launch (start us, length us, event | category | flops | bytes accessed | tf_op | source)
XLA Modules:
  0.0 1106.0 jit_solution(3419291461261815503)
XLA Ops:
  8.1 2.5 pad_maximum_fusion.2.refs_2_
  12.8 344.7 %shard_map.237 = (bf16[2,2,4,2,64,6400]{5,4,3,2,1,0:T(8,128)(2,1)}, bf16[2,2,4,2,64,2048]{5,4,3,2,1,0:T(8,128)(2,1)}, bf16[2,2,4,2,64,11264]{5,4,3,2,1,0:T(8,128)(2,1)}) custom-call(bf16[64,6400]{1,0:T(8,128)(2,1)} %fusion.8.refs_0_, bf16[64,2048]{1,0:T(8,128)(2,1)} %refs_1_.1, bf16[64,11264]{1,0:T(8,128)(2,1)} %pad_maximum_fusion.2.refs_2_), custom_call_target="tpu_custom_call" | custom-call | tf_op jit(solution)/shard_map/pallas_call | solution.py:669
  366.8 17.9 %fusion.48.refs_0_.refs_1_ = f32[384,6400]{1,0:T(8,128)} fusion(bf16[384,2048]{1,0:T(8,128)(2,1)S(1)} %bitcast.387, bf16[2048,6400]{1,0:T(8,128)(2,1)} %bitcast.403), kind=kOutput, calls=%fused_computation.158 | convolution fusion | flops 10066329600 | bytes 37617664 | tf_op jit(solution)/shard_map/dot_general | solution.py:30
  385.6 10.0 shard_map.238
  397.6 18.9 %all_gather.13 = bf16[8,6,2048]{2,1,0:T(8,128)(2,1)S(1)} all-gather(bf16[1,6,2048]{2,1,0:T(8,128)(2,1)S(1)} %pad_maximum_fusion.3), channel_id=1, replica_groups=mesh['dp'=4,'seq'=8] {'seq'}, dimensions={0}, use_global_device_ids=true | all-gather | bytes 221184 | tf_op jit(solution)/shard_map/all_gather | solution.py:162
  417.4 3.9 multiply_reduce_fusion.7
  421.3 3.1 multiply_convert_fusion.8
  424.5 5.1 multiply_reduce_fusion.6
  429.6 29.4 %fusion.40 = f32[384,11264]{1,0:T(8,128)} fusion(bf16[2048,11264]{1,0:T(8,128)(2,1)} %bitcast.409, f32[384,2048]{1,0:T(8,128)} %get-tuple-element.161, f32[2048]{0:T(1024)S(1)} %bitcast.393, f32[384]{0:T(512)S(1)} %add_rsqrt_fusion), kind=kOutput, calls=%fused_computation.153 | convolution fusion | flops 17719099392 | bytes 66594304 | tf_op jit(solution)/shard_map/dot_general | solution.py:30
  459.0 9.5 multiply_convert_fusion.2
  468.5 18.9 %convolution_convert_fusion = bf16[5632,2048]{1,0:T(8,128)(2,1)} fusion(bf16[384,5632]{1,0:T(8,128)(2,1)} %multiply_convert_fusion.2, bf16[384,2048]{1,0:T(8,128)(2,1)} %bitcast_convert_fusion), kind=kOutput, calls=%fused_computation | convolution fusion | flops 8869904384 | bytes 28966912 | tf_op jit(solution)/shard_map/dot_general | solution.py:40
  487.5 22.8 %all-gather.4.cloned.1.call-done = bf16[5632,2048]{1,0:T(8,128)(2,1)} async-done(((bf16[176,2048]{1,0:T(8,128)(2,1)}), bf16[5632,2048]{1,0:T(8,128)(2,1)}) %all-gather.4.cloned.1.call-update) | async-done | bytes 23068688 | tf_op jit(solution)/shard_map/all_gather | solution.py:691
  510.3 11.4 %copy.108.refs_1_ = bf16[2048,384]{1,0:T(8,128)(2,1)} copy(bf16[2048,384]{0,1:T(8,128)(2,1)} %bitcast.384) | data formatting | bytes 3145728 | tf_op jit(solution)/shard_map/transpose | solution.py:849
  523.8 3.5 slice_add_fusion
  529.4 22.2 %multiply_convert_fusion.1 = (bf16[384,5632]{1,0:T(8,128)(2,1)}, bf16[384,5632]{1,0:T(8,128)(2,1)}) fusion(f32[384,11264]{1,0:T(8,128)} %fusion.40, bf16[5632,2048]{1,0:T(8,128)(2,1)} %all-gather.4.cloned.1.call-done, bf16[384,2048]{1,0:T(8,128)(2,1)} %bitcast_convert_fusion), kind=kOutput, calls=%fused_computation.4 | convolution fusion | flops 8886484992 | bytes 50593792 | tf_op jit(solution)/shard_map/dot_general | solution.py:34
  551.7 26.0 %fusion.41 = f32[384,2048]{1,0:T(8,128)} fusion(bf16[2048,11264]{1,0:T(8,128)(2,1)} %bitcast.410, bf16[384,5632]{1,0:T(8,128)(2,1)} %get-tuple-element.148, bf16[384,5632]{1,0:T(8,128)(2,1)} %get-tuple-element.147), kind=kOutput, calls=%fused_computation.154 | convolution fusion | flops 17734041600 | bytes 57933824 | tf_op jit(solution)/shard_map/dot_general | solution.py:34
  577.7 5.1 multiply_reduce_fusion
  582.8 5.0 fusion.46
  587.8 7.7 multiply_reduce_fusion.1
  595.6 2.6 copy.109.refs_2_
  598.1 5.5 subtract_multiply_fusion
  603.7 11.4 %shard_map.239 = (f32[384,2048]{1,0:T(8,128)}, f32[384,2048]{1,0:T(8,128)}, f32[3,2048]{1,0:T(4,128)}) custom-call(f32[384,2048]{1,0:T(8,128)} %get-tuple-element.150.refs_0_, f32[384,6400]{1,0:T(8,128)} %fusion.48.refs_0_.refs_1_, f32[1,2048]{1,0:T(1,128)} %get-tuple-element.156.refs_2_, f32[384,128]{1,0:T(8,128)} %broadcast_in_dim.9.refs_3_), custom_call_target="tpu_custom_call" | custom-call | tf_op jit(solution)/shard_map/pallas_call | solution.py:146
  615.8 14.9 %all-gather.1 = bf16[8,3,2048]{2,1,0:T(4,128)(2,1)S(1)} all-gather(bf16[1,3,2048]{2,1,0:T(4,128)(2,1)S(1)} %convert_bitcast_fusion), channel_id=2, replica_groups=mesh['dp'=4,'seq'=8] {'seq'}, dimensions={0}, use_global_device_ids=true | all-gather | bytes 110592 | tf_op jit(solution)/shard_map/all_gather | solution.py:162
  631.8 7.2 fusion.43
  639.0 4.1 multiply_convert_fusion.5
  643.1 19.0 %multiply_reduce_fusion.2 = (bf16[2048]{0:T(1024)(128)(2,1)S(1)}, f32[384]{0:T(512)S(1)}, bf16[384,2048]{1,0:T(8,128)(2,1)}, f32[384,2048]{1,0:T(8,128)}) fusion(f32[3,1,128,2048]{3,2,1,0:T(8,128)S(1)} %copy-done.2, f32[384]{0:T(512)S(1)} %copy-done.21, f32[2048]{0:T(1024)S(1)} %bitcast.397, bf16[2048,6400]{1,0:T(8,128)(2,1)} %bitcast.404, ...), kind=kOutput, calls=%fused_computation.26 | convolution fusion | flops 10092279808 | bytes 38825472 | tf_op jit(solution)/shard_map/dot_general | solution.py:34
  665.3 2.7 copy.107.refs_0_
  667.9 7.8 pad_maximum_fusion.refs_5_
  675.8 5.7 maximum_maximum_fusion.refs_3_
  681.5 385.9 %shard_map.240 = (f32[64,2048]{1,0:T(8,128)}, f32[64,2048]{1,0:T(8,128)}, f32[64,2048]{1,0:T(8,128)}, f32[64,2048]{1,0:T(8,128)}, f32[64,5632]{1,0:T(8,128)}, /*index=5*/f32[64,5632]{1,0:T(8,128)}, f32[64,512]{1,0:T(8,128)}) custom-call(bf16[2048,384]{1,0:T(8,128)(2,1)} %copy.107.refs_0_, bf16[2048,384]{1,0:T(8,128)(2,1)} %copy.108.refs_1_, ...), custom_call_target="tpu_custom_call" | custom-call | tf_op jit(solution)/shard_map/pallas_call | solution.py:495
  1069.1 5.4 multiply_add_fusion
  1074.5 16.2 %convolution_add_fusion = f32[384,2048]{1,0:T(8,128)} fusion(f32[384,2048]{1,0:T(8,128)S(1)} %copy-done.7, bf16[384,5632]{1,0:T(8,128)(2,1)} %multiply_convert_fusion.2, bf16[5632,2048]{1,0:T(8,128)(2,1)} %all-gather.4.cloned.1.call-done), kind=kOutput, calls=%fused_computation.47 | convolution fusion | flops 8859156480 | bytes 33685504 | tf_op jit(solution)/shard_map/dot_general | solution.py:30
  (117 shorter events, 35.0 us)
Async XLA Ops:
  7.2 503.0 %all-gather.4.cloned.1.call-start = ((), (), s32[]{:S(2)}) async-start(), calls=%async_computation.1 | async-start | bytes 23789568 | tf_op jit(solution)/shard_map/all_gather | solution.py:691
  10.6 350.1 %copy-start.22 = (s32[3,1,128]{2,1,0:T(1,128)S(1)}, s32[3,1,128]{2,1,0:T(1,128)}, u32[]{:S(2)}) copy-start(s32[3,1,128]{2,1,0:T(1,128)} %param.15) | copy-start | bytes 4612
  10.6 352.6 %copy-start = (f32[3,1,128,2048]{3,2,1,0:T(8,128)S(1)}, f32[3,1,128,2048]{3,2,1,0:T(8,128)}, u32[]{:S(2)}) copy-start(f32[3,1,128,2048]{3,2,1,0:T(8,128)} %param.14) | copy-start | bytes 9437188
  360.7 730.1 %reduce-scatter.2.cloned.1.call-start = ((), (), s32[]{:S(2)}) async-start(), calls=%async_computation.2 | async-start | bytes 23789568 | tf_op jit(solution)/shard_map/reduce_scatter | solution.py:695
  360.8 23.9 %collective-permute-start = (s32[3,1]{1,0:T(4,128)S(1)}, s32[3,1]{1,0:T(4,128)S(1)}, u32[]{:S(2)}, u32[]{:S(2)}) collective-permute-start(s32[3,1]{1,0:T(4,128)S(1)} %slice.152), channel_id=1, source_target_pairs={{0,1},{1,2},{2,3},{3,4},{4,5},{5,6},{6,7},{8,9},{9,10},{10,11},{11... | collective-permute-start | bytes 44 | tf_op jit(solution)/shard_map/ppermute | solution.py:751
  363.1 1.9 copy-start.3
  365.0 1.7 copy-start.17
  384.8 10.8 copy-start.19
  416.4 8.0 slice-start
  416.5 0.8 copy-start.10
  417.4 7.1 slice-start.1
  421.3 3.2 copy-start.1
  424.4 5.2 copy-start.9
  577.7 5.1 copy-start.4
  577.7 5.1 copy-start.6
  577.7 10.1 slice-start.2
  582.8 5.0 slice-start.3
  587.8 7.7 copy-start.8
  603.7 28.1 %copy-start.5 = (f32[3,128,2048]{2,1,0:T(8,128)S(1)}, f32[3,128,2048]{2,1,0:T(8,128)}, u32[]{:S(2)}) copy-start(f32[3,128,2048]{2,1,0:T(8,128)} %pad_maximum_fusion.1) | copy-start | bytes 9437188
  603.7 28.2 %copy-start.20 = (f32[384]{0:T(512)S(1)}, f32[384]{0:T(512)}, u32[]{:S(2)}) copy-start(f32[384]{0:T(512)} %copy-done.19) | copy-start | bytes 4612
  639.0 4.1 copy-start.2
  639.0 4.1 copy-start.18
  639.0 4.1 copy-start.21
  1069.1 5.4 copy-start.7
  1074.5 18.8 %copy-start.16 = (f32[64,2048]{1,0:T(8,128)S(1)}, f32[64,2048]{1,0:T(8,128)}, u32[]{:S(2)}) copy-start(f32[64,2048]{1,0:T(8,128)} %get-tuple-element.182) | copy-start | bytes 1572868
  1090.7 3.4 copy-start.15
  1090.7 4.2 copy-start.14
  1090.7 5.0 copy-start.13
  1090.7 5.7 copy-start.12
  1094.1 3.5 copy-start.11
Sparse Core Ops, SparseCore 0:
  360.8 149.3 all-gather.3
  512.5 265.6 reduce-scatter.1

commit v4 on v3

--- a/solution.py
+++ b/solution.py
@@ -12,8 +12,9 @@
 LANES = 128
 SUB = 8
 MESH = pl.DeviceIdType.MESH
-SLOTS = 2
+SLOTS = 3
 AHEAD = 12
+LAG = 2
 EXTRA = 256
 
 
@@ -220,8 +221,10 @@
     vec = take(1)[0] if has_vec else None
     outs = take(len(spans))
     (part, core_in, one_a, one_b, in_a, in_b, two_a, two_b, far_a, far_b, three, line_in) = take(12)
+    (mid_a, mid_b, four_a, four_b, last_a, last_b) = take(6)
     (core_s, core_r, ya_s, ya_r, xb_s, xb_r, xa_s, xa_r, yb_s, yb_r, z_s, z_r) = take(12)
-    (core_f, ya_f, xb_f, xa_f, yb_f, z_f) = take(6)
+    (ma_s, ma_r, mb_s, mb_r, la_s, la_r, lb_s, lb_r) = take(8)
+    (core_f, ya_f, xb_f, xa_f, yb_f, z_f, ma_f, mb_f, la_f, lb_f) = take(10)
     here = locate(dims)
     y, x, z, c = here
     greet(dims, here)
@@ -232,86 +235,73 @@
             src_ref=src, dst_ref=dst, send_sem=ss, recv_sem=rs, device_id=peer, device_id_type=MESH
         )
 
+    late_total = total // 3
+    early_total = total - late_total
+
+    def is_late(t):
+        return lax.rem(t, 3) == 2
+
+    def late_index(t):
+        return lax.div(t, 3)
+
+    def early_index(t):
+        return 2 * lax.div(t, 3) + lax.rem(t, 3)
+
+    x_hops = [(k - 1, hop(x, k, X), hop(x, X - k, X)) for k in range(1, X)]
+    y_hops = [(k - 1, hop(y, k, Y), hop(y, Y - k, Y)) for k in range(1, Y)]
+    z_hops = [(k - 1, hop(z, k, Z), hop(z, Z - k, Z)) for k in range(1, Z)]
+    at_x = lambda i: device(dims, y, i, z, c)
+    at_y = lambda i: device(dims, i, x, z, c)
+    at_z = lambda i: device(dims, y, x, i, c)
+
+    def along(hops, at, piece, landing, ss, rs, free, s):
+        return [
+            (
+                send(piece(to), landing.at[s, n], ss.at[s, n], rs.at[s, n], at(to)),
+                free.at[n],
+                at(giver),
+            )
+            for n, to, giver in hops
+        ]
+
     def core_copies(t):
         s = lax.rem(t, SLOTS)
-        return [
-            (
-                send(part.at[s, 1 - c], core_in.at[s], core_s.at[s], core_r.at[s],
-                     device(dims, y, x, z, 1 - c)),
-                core_f.at[0],
-                device(dims, y, x, z, 1 - c),
-            )
-        ]
+        peer = device(dims, y, x, z, 1 - c)
+        copy = send(part.at[s, 1 - c], core_in.at[s], core_s.at[s], core_r.at[s], peer)
+        return [(copy, core_f.at[0], peer)]
 
     def first_copies(t):
         s = lax.rem(t, SLOTS)
-        out = []
-        for k in range(1, Y):
-            to, frm = hop(y, k, Y), hop(y, Y - k, Y)
-            out.append(
-                (
-                    send(one_a.at[s, to], in_a.at[s, k - 1], ya_s.at[s, k - 1], ya_r.at[s, k - 1],
-                         device(dims, to, x, z, c)),
-                    ya_f.at[k - 1],
-                    device(dims, frm, x, z, c),
-                )
-            )
-        for k in range(1, X):
-            to, frm = hop(x, k, X), hop(x, X - k, X)
-            out.append(
-                (
-                    send(one_b.at[s, to], in_b.at[s, k - 1], xb_s.at[s, k - 1], xb_r.at[s, k - 1],
-                         device(dims, y, to, z, c)),
-                    xb_f.at[k - 1],
-                    device(dims, y, frm, z, c),
-                )
-            )
-        return out
+        return along(
+            y_hops, at_y, lambda to: one_a.at[s, to], in_a, ya_s, ya_r, ya_f, s
+        ) + along(x_hops, at_x, lambda to: one_b.at[s, to], in_b, xb_s, xb_r, xb_f, s)
 
     def second_copies(t):
-        s = lax.rem(t, SLOTS)
-        out = []
-        for k in range(1, X):
-            to, frm = hop(x, k, X), hop(x, X - k, X)
-            out.append(
-                (
-                    send(two_a.at[s, to], far_a.at[s, k - 1], xa_s.at[s, k - 1], xa_r.at[s, k - 1],
-                         device(dims, y, to, z, c)),
-                    xa_f.at[k - 1],
-                    device(dims, y, frm, z, c),
-                )
-            )
-        for k in range(1, Y):
-            to, frm = hop(y, k, Y), hop(y, Y - k, Y)
-            out.append(
-                (
-                    send(two_b.at[s, to], far_b.at[s, k - 1], yb_s.at[s, k - 1], yb_r.at[s, k - 1],
-                         device(dims, to, x, z, c)),
-                    yb_f.at[k - 1],
-                    device(dims, frm, x, z, c),
-                )
-            )
-        return out
+        s, r = lax.rem(t, SLOTS), lax.rem(early_index(t), SLOTS)
+        return along(
+            x_hops, at_x, lambda to: two_a.at[s, to], far_a, xa_s, xa_r, xa_f, r
+        ) + along(y_hops, at_y, lambda to: two_b.at[s, to], far_b, yb_s, yb_r, yb_f, r)
+
+    def middle_copies(t):
+        s, r = lax.rem(t, SLOTS), lax.rem(late_index(t), SLOTS)
+        return along(
+            z_hops, at_z, lambda to: two_a.at[s, :, to], mid_a, ma_s, ma_r, ma_f, r
+        ) + along(z_hops, at_z, lambda to: two_b.at[s, :, to], mid_b, mb_s, mb_r, mb_f, r)
 
     def line_copies(t):
-        s = lax.rem(t, SLOTS)
-        out = []
-        for k in range(1, Z):
-            to, frm = hop(z, k, Z), hop(z, Z - k, Z)
-            out.append(
-                (
-                    send(three.at[s, to], line_in.at[s, k - 1], z_s.at[s, k - 1], z_r.at[s, k - 1],
-                         device(dims, y, x, to, c)),
-                    z_f.at[k - 1],
-                    device(dims, y, x, frm, c),
-                )
-            )
-        return out
-
-    def begin(copies, t):
+        s, r = lax.rem(t, SLOTS), lax.rem(early_index(t), SLOTS)
+        return along(z_hops, at_z, lambda to: three.at[s, to], line_in, z_s, z_r, z_f, r)
+
+    def last_copies(t):
+        s, r = lax.rem(t, SLOTS), lax.rem(late_index(t), SLOTS)
+        return along(
+            x_hops, at_x, lambda to: four_a.at[s, to], last_a, la_s, la_r, la_f, r
+        ) + along(y_hops, at_y, lambda to: four_b.at[s, to], last_b, lb_s, lb_r, lb_f, r)
+
+    def begin(copies, index):
         for copy, free, _ in copies:
 
-            @pl.when(t >= SLOTS)
+            @pl.when(index >= SLOTS)
             def _():
                 pl.semaphore_wait(free, 1)
 
@@ -321,12 +311,18 @@
         for copy, _, _ in copies:
             copy.wait()
 
-    def release(copies, t):
+    def release(copies, index, count):
         for _, free, giver in copies:
 
-            @pl.when(t + SLOTS < total)
+            @pl.when(index + SLOTS < count)
             def _():
                 pl.semaphore_signal(free, inc=1, device_id=giver, device_id_type=MESH)
+
+    def summed(own, landing, r, hops):
+        value = own.astype(f32)
+        for n, _, _ in hops:
+            value = value + landing[r, n].astype(f32)
+        return value
 
     def produce(t):
         s = lax.rem(t, SLOTS)
@@ -381,7 +377,7 @@
             produce(t)
             begin(core_copies(t), t)
 
-        u = t - 1
+        u = t - 2
 
         @pl.when(jnp.logical_and(u >= 0, u < total))
         def _():
@@ -398,65 +394,89 @@
                 return 0
 
             lax.fori_loop(0, Y * X, block, 0)
-            release(copies, u)
+            release(copies, u, total)
             begin(first_copies(u), u)
 
-        v = t - 2
-
-        @pl.when(jnp.logical_and(v >= 0, v < total))
+        v = t - 4
+        inside = jnp.logical_and(v >= 0, v < total)
+
+        @pl.when(inside)
         def _():
             s = lax.rem(v, SLOTS)
             copies = first_copies(v)
             arrive(copies)
-            value = one_a[s, y].astype(f32)
-            for k in range(Y - 1):
-                value = value + in_a[s, k].astype(f32)
-            two_a[s] = value.astype(low)
-            value = one_b[s, x].astype(f32)
-            for k in range(X - 1):
-                value = value + in_b[s, k].astype(f32)
-            two_b[s] = value.astype(low)
-            release(copies, v)
-            begin(second_copies(v), v)
-
-        w = t - 3
-
-        @pl.when(jnp.logical_and(w >= 0, w < total))
+            two_a[s] = summed(one_a[s, y], in_a, s, y_hops).astype(low)
+            two_b[s] = summed(one_b[s, x], in_b, s, x_hops).astype(low)
+            release(copies, v, total)
+
+        @pl.when(jnp.logical_and(inside, jnp.logical_not(is_late(v))))
         def _():
-            s = lax.rem(w, SLOTS)
+            begin(second_copies(v), early_index(v))
+
+        @pl.when(jnp.logical_and(inside, is_late(v)))
+        def _():
+            begin(middle_copies(v), late_index(v))
+
+        w = t - 6
+        inside = jnp.logical_and(w >= 0, w < total)
+
+        @pl.when(jnp.logical_and(inside, jnp.logical_not(is_late(w))))
+        def _():
+            s, index = lax.rem(w, SLOTS), early_index(w)
+            r = lax.rem(index, SLOTS)
             copies = second_copies(w)
             arrive(copies)
-            value = two_a[s, x].astype(f32)
-            for k in range(X - 1):
-                value = value + far_a[s, k].astype(f32)
-            three[s, :, :, :half] = value.astype(low)
-            value = two_b[s, y].astype(f32)
-            for k in range(Y - 1):
-                value = value + far_b[s, k].astype(f32)
-            three[s, :, :, half:] = value.astype(low)
-            release(copies, w)
-            begin(line_copies(w), w)
-
-        q = t - 4
-
-        @pl.when(q >= 0)
+            three[s, :, :, :half] = summed(two_a[s, x], far_a, r, x_hops).astype(low)
+            three[s, :, :, half:] = summed(two_b[s, y], far_b, r, y_hops).astype(low)
+            release(copies, index, early_total)
+            begin(line_copies(w), index)
+
+        @pl.when(jnp.logical_and(inside, is_late(w)))
         def _():
-            s = lax.rem(q, SLOTS)
+            s, index = lax.rem(w, SLOTS), late_index(w)
+            r = lax.rem(index, SLOTS)
+            copies = middle_copies(w)
+            arrive(copies)
+            four_a[s] = summed(two_a[s, :, z], mid_a, r, z_hops).astype(low)
+            four_b[s] = summed(two_b[s, :, z], mid_b, r, z_hops).astype(low)
+            release(copies, index, late_total)
+            begin(last_copies(w), index)
+
+        q = t - 8
+
+        def store(first, last, value):
+            for number, (_, low_t, high_t) in enumerate(spans):
+
+                @pl.when(jnp.logical_and(q >= low_t, q < high_t))
+                def _():
+                    start = pl.multiple_of((q - low_t) * wide + first, half)
+                    outs[number][:, pl.ds(start, last - first)] = value
+
+        @pl.when(jnp.logical_and(q >= 0, jnp.logical_not(is_late(q))))
+        def _():
+            s, index = lax.rem(q, SLOTS), early_index(q)
+            r = lax.rem(index, SLOTS)
             copies = line_copies(q)
             arrive(copies)
-            value = three[s, z].astype(f32)
-            for k in range(Z - 1):
-                value = value + line_in[s, k].astype(f32)
-            release(copies, q)
-            for index, (_, low_t, high_t) in enumerate(spans):
-
-                @pl.when(jnp.logical_and(q >= low_t, q < high_t))
-                def _():
-                    outs[index][:, pl.ds(pl.multiple_of((q - low_t) * wide, wide), wide)] = value
+            value = summed(three[s, z], line_in, r, z_hops)
+            release(copies, index, early_total)
+            store(0, wide, value)
+
+        @pl.when(jnp.logical_and(q >= 0, is_late(q)))
+        def _():
+            s, index = lax.rem(q, SLOTS), late_index(q)
+            r = lax.rem(index, SLOTS)
+            copies = last_copies(q)
+            arrive(copies)
+            value_a = summed(four_a[s, x], last_a, r, x_hops)
+            value_b = summed(four_b[s, y], last_b, r, y_hops)
+            release(copies, index, late_total)
+            store(0, half, value_a)
+            store(half, wide, value_b)
 
         return 0
 
-    lax.fori_loop(0, total + 4, step, 0)
+    lax.fori_loop(0, total + 8, step, 0)
 
 
 def scatter_call(dims, depth, wide, pairs, widths, vec, collective_id):
@@ -488,10 +508,18 @@
         vmem(y1, Z, depth, half),
         vmem(Z, depth, wide),
         vmem(z1, depth, wide),
+        vmem(z1, X, depth, half),
+        vmem(z1, Y, depth, half),
+        vmem(X, depth, half),
+        vmem(Y, depth, half),
+        vmem(x1, depth, half),
+        vmem(y1, depth, half),
     ]
     scratch += [dma(), dma()]
     scratch += [dma(y1), dma(y1), dma(x1), dma(x1), dma(x1), dma(x1), dma(y1), dma(y1), dma(z1), dma(z1)]
+    scratch += [dma(z1), dma(z1), dma(z1), dma(z1), dma(x1), dma(x1), dma(y1), dma(y1)]
     scratch += [reg(1), reg(y1), reg(x1), reg(x1), reg(y1), reg(z1)]
+    scratch += [reg(z1), reg(z1), reg(x1), reg(y1)]
     return pl.pallas_call(
         functools.partial(
             scatter_kernel, dims, depth, wide, len(pairs), spans, vec is not None
@@ -599,66 +627,51 @@
     ]
     for copy in own:
         copy.start()
-
-    for i in range(n):
-        total = counts[i]
-
-        def either(t, inside, one, other, act):
-            late = lax.rem(bases[i] + t, 3) == 2
+    for copy in own:
+        copy.wait()
+    total = sum(counts)
+
+    def start(copy):
+        copy.start()
+
+    def wait(copy):
+        copy.wait()
+
+    def either(g, one, other, act):
+        late = lax.rem(g, 3) == 2
+        for i in range(n):
+            inside = jnp.logical_and(g >= bases[i], g < bases[i] + counts[i])
 
             @pl.when(jnp.logical_and(inside, jnp.logical_not(late)))
             def _():
-                for copy in one(i, t):
+                for copy in one(i, g - bases[i]):
                     act(copy)
 
             @pl.when(jnp.logical_and(inside, late))
             def _():
-                for copy in other(i, t):
+                for copy in other(i, g - bases[i]):
                     act(copy)
 
-        def start(copy):
-            copy.start()
-
-        def wait(copy):
-            copy.wait()
-
-        def step(t, _):
-            either(t, t < total, line_copies, own_copies, start)
-
-            u = t - 2
-            inside = jnp.logical_and(u >= 0, u < total)
-            either(u, inside, line_copies, own_copies, wait)
-            either(u, inside, first_copies, middle_copies, start)
-
-            v = t - 4
-            inside = jnp.logical_and(v >= 0, v < total)
-            either(v, inside, first_copies, middle_copies, wait)
-
-            @pl.when(inside)
+    def every(g, one, act):
+        for i in range(n):
+
+            @pl.when(jnp.logical_and(g >= bases[i], g < bases[i] + counts[i]))
             def _():
-                for copy in second_copies(i, v):
-                    copy.start()
-
-            w = t - 6
-
-            @pl.when(jnp.logical_and(w >= 0, w < total))
-            def _():
-                for copy in second_copies(i, w):
-                    copy.wait()
-                for copy in core_copies(i, w):
-                    copy.start()
-
-            q = t - 8
-
-            @pl.when(q >= 0)
-            def _():
-                for copy in core_copies(i, q):
-                    copy.wait()
-
-            return 0
-
-        own[i].wait()
-        lax.fori_loop(0, total + 8, step, 0)
+                for copy in one(i, g - bases[i]):
+                    act(copy)
+
+    def step(g, _):
+        either(g, line_copies, own_copies, start)
+        either(g - LAG, line_copies, own_copies, wait)
+        either(g - LAG, first_copies, middle_copies, start)
+        either(g - 2 * LAG, first_copies, middle_copies, wait)
+        every(g - 2 * LAG, second_copies, start)
+        every(g - 3 * LAG, second_copies, wait)
+        every(g - 3 * LAG, core_copies, start)
+        every(g - 4 * LAG, core_copies, wait)
+        return 0
+
+    lax.fori_loop(0, total + 4 * LAG, step, 0)
 
 
 def gather_call(dims, shards, wides, collective_id):

time: 1110 us -> 1080 us (0.973)
  Pallas kernels: 752 us -> 722 us
    pallas_call x1, Pallas kernels: 345 us -> 322 us  [gather_call(): pl.pallas_call(functools.partial(gather_kernel, dims, wides), out_shape=[...]
where the time goes in v4:
time: 1080 us; the launch traced here: 1070 us
  Pallas kernels  722 us (67%)
  matrix products  163 us (15%)
  other arithmetic  82.6 us (8%)
  local copies, waits for them, and re-layouts  34.9 us (3%)
  blocking collectives  31.3 us (3%)
  waiting for transfers between devices  22.2 us (2%)
  between operations  14.9 us (1%)
    pallas_call x1, Pallas kernels, scatter_call(): pl.pallas_call(functools.partial(scatter_kernel, dims, depth, wide, len(p...  379 us
    pallas_call x1, Pallas kernels, gather_call(): pl.pallas_call(functools.partial(gather_kernel, dims, wides), out_shape=[...  322 us
    dot_general x4, matrix products, contract_last(): lax.dot_general(left, right, (((1,), (1,)), ((), ())), preferred_element_...  75 us
    dot_general x4, matrix products, dot(): return jnp.dot(left, right, preferred_element_type=jnp.float32)  68.9 us
    all_gather x2, blocking collectives, exchange(): return lax.all_gather(value.astype(jnp.bfloat16), 'seq').astype(jnp.float32)  31.3 us
    all_gather x1, waiting for transfers between devices, gather_all(): return lax.all_gather(shard, ALL, axis=0, tiled=True)  22.2 us
  transfers between devices with their start and end apart: 3, of which 1 were waited for; matrix products, arithmetic and copies ran while one was open for 24% of the time, Pallas kernels for 37%

profile of v4, /device:TPU:0, one launch (start us, length us, event | category | flops | bytes accessed | tf_op | source)
XLA Modules:
  0.0 1072.5 jit_solution(13464459943235554047)
XLA Ops:
  8.1 2.5 pad_maximum_fusion.2.refs_2_
  12.8 321.5 %shard_map.237 = (bf16[2,2,4,2,64,6400]{5,4,3,2,1,0:T(8,128)(2,1)}, bf16[2,2,4,2,64,2048]{5,4,3,2,1,0:T(8,128)(2,1)}, bf16[2,2,4,2,64,11264]{5,4,3,2,1,0:T(8,128)(2,1)}) custom-call(bf16[64,6400]{1,0:T(8,128)(2,1)} %fusion.8.refs_0_, bf16[64,2048]{1,0:T(8,128)(2,1)} %refs_1_.1, bf16[64,11264]{1,0:T(8,128)(2,1)} %pad_maximum_fusion.2.refs_2_), custom_call_target="tpu_custom_call" | custom-call | tf_op jit(solution)/shard_map/pallas_call | solution.py:682
  343.6 18.5 %fusion.48.refs_0_.refs_1_ = f32[384,6400]{1,0:T(8,128)} fusion(bf16[384,2048]{1,0:T(8,128)(2,1)S(1)} %bitcast.387, bf16[2048,6400]{1,0:T(8,128)(2,1)} %bitcast.403), kind=kOutput, calls=%fused_computation.158 | convolution fusion | flops 10066329600 | bytes 37617664 | tf_op jit(solution)/shard_map/dot_general | solution.py:31
  362.9 10.0 shard_map.238
  374.9 16.5 %all_gather.13 = bf16[8,6,2048]{2,1,0:T(8,128)(2,1)S(1)} all-gather(bf16[1,6,2048]{2,1,0:T(8,128)(2,1)S(1)} %pad_maximum_fusion.3), channel_id=1, replica_groups=mesh['dp'=4,'seq'=8] {'seq'}, dimensions={0}, use_global_device_ids=true | all-gather | bytes 221184 | tf_op jit(solution)/shard_map/all_gather | solution.py:163
  392.3 3.9 multiply_reduce_fusion.7
  396.2 3.0 multiply_convert_fusion.8
  399.3 5.1 multiply_reduce_fusion.6
  404.4 29.1 %fusion.40 = f32[384,11264]{1,0:T(8,128)} fusion(bf16[2048,11264]{1,0:T(8,128)(2,1)} %bitcast.409, f32[384,2048]{1,0:T(8,128)} %get-tuple-element.161, f32[2048]{0:T(1024)S(1)} %bitcast.393, f32[384]{0:T(512)S(1)} %add_rsqrt_fusion), kind=kOutput, calls=%fused_computation.153 | convolution fusion | flops 17719099392 | bytes 66594304 | tf_op jit(solution)/shard_map/dot_general | solution.py:31
  433.5 9.5 multiply_convert_fusion.2
  443.1 18.7 %convolution_convert_fusion = bf16[5632,2048]{1,0:T(8,128)(2,1)} fusion(bf16[384,5632]{1,0:T(8,128)(2,1)} %multiply_convert_fusion.2, bf16[384,2048]{1,0:T(8,128)(2,1)} %bitcast_convert_fusion), kind=kOutput, calls=%fused_computation | convolution fusion | flops 8869904384 | bytes 28966912 | tf_op jit(solution)/shard_map/dot_general | solution.py:41
  461.7 22.2 %all-gather.4.cloned.1.call-done = bf16[5632,2048]{1,0:T(8,128)(2,1)} async-done(((bf16[176,2048]{1,0:T(8,128)(2,1)}), bf16[5632,2048]{1,0:T(8,128)(2,1)}) %all-gather.4.cloned.1.call-update) | async-done | bytes 23068688 | tf_op jit(solution)/shard_map/all_gather | solution.py:704
  484.0 11.4 %copy.108.refs_1_ = bf16[2048,384]{1,0:T(8,128)(2,1)} copy(bf16[2048,384]{0,1:T(8,128)(2,1)} %bitcast.384) | data formatting | bytes 3145728 | tf_op jit(solution)/shard_map/transpose | solution.py:862
  497.5 3.5 slice_add_fusion
  503.1 22.3 %multiply_convert_fusion.1 = (bf16[384,5632]{1,0:T(8,128)(2,1)}, bf16[384,5632]{1,0:T(8,128)(2,1)}) fusion(f32[384,11264]{1,0:T(8,128)} %fusion.40, bf16[5632,2048]{1,0:T(8,128)(2,1)} %all-gather.4.cloned.1.call-done, bf16[384,2048]{1,0:T(8,128)(2,1)} %bitcast_convert_fusion), kind=kOutput, calls=%fused_computation.4 | convolution fusion | flops 8886484992 | bytes 50593792 | tf_op jit(solution)/shard_map/dot_general | solution.py:35
  525.4 26.0 %fusion.41 = f32[384,2048]{1,0:T(8,128)} fusion(bf16[2048,11264]{1,0:T(8,128)(2,1)} %bitcast.410, bf16[384,5632]{1,0:T(8,128)(2,1)} %get-tuple-element.148, bf16[384,5632]{1,0:T(8,128)(2,1)} %get-tuple-element.147), kind=kOutput, calls=%fused_computation.154 | convolution fusion | flops 17734041600 | bytes 57933824 | tf_op jit(solution)/shard_map/dot_general | solution.py:35
  551.4 5.1 multiply_reduce_fusion
  556.5 5.0 fusion.46
  561.5 7.7 multiply_reduce_fusion.1
  569.2 2.6 copy.109.refs_2_
  571.8 5.5 subtract_multiply_fusion
  577.4 11.4 %shard_map.239 = (f32[384,2048]{1,0:T(8,128)}, f32[384,2048]{1,0:T(8,128)}, f32[3,2048]{1,0:T(4,128)}) custom-call(f32[384,2048]{1,0:T(8,128)} %get-tuple-element.150.refs_0_, f32[384,6400]{1,0:T(8,128)} %fusion.48.refs_0_.refs_1_, f32[1,2048]{1,0:T(1,128)} %get-tuple-element.156.refs_2_, f32[384,128]{1,0:T(8,128)} %broadcast_in_dim.9.refs_3_), custom_call_target="tpu_custom_call" | custom-call | tf_op jit(solution)/shard_map/pallas_call | solution.py:147
  589.5 14.9 %all-gather.1 = bf16[8,3,2048]{2,1,0:T(4,128)(2,1)S(1)} all-gather(bf16[1,3,2048]{2,1,0:T(4,128)(2,1)S(1)} %convert_bitcast_fusion), channel_id=2, replica_groups=mesh['dp'=4,'seq'=8] {'seq'}, dimensions={0}, use_global_device_ids=true | all-gather | bytes 110592 | tf_op jit(solution)/shard_map/all_gather | solution.py:163
  605.5 7.2 fusion.43
  612.7 4.1 multiply_convert_fusion.5
  616.8 19.0 %multiply_reduce_fusion.2 = (bf16[2048]{0:T(1024)(128)(2,1)S(1)}, f32[384]{0:T(512)S(1)}, bf16[384,2048]{1,0:T(8,128)(2,1)}, f32[384,2048]{1,0:T(8,128)}) fusion(f32[3,1,128,2048]{3,2,1,0:T(8,128)S(1)} %copy-done.2, f32[384]{0:T(512)S(1)} %copy-done.21, f32[2048]{0:T(1024)S(1)} %bitcast.397, bf16[2048,6400]{1,0:T(8,128)(2,1)} %bitcast.404, ...), kind=kOutput, calls=%fused_computation.26 | convolution fusion | flops 10092279808 | bytes 38825472 | tf_op jit(solution)/shard_map/dot_general | solution.py:35
  638.9 2.6 copy.107.refs_0_
  641.6 7.8 pad_maximum_fusion.refs_5_
  649.4 5.7 maximum_maximum_fusion.refs_3_
  655.2 378.8 %shard_map.240 = (f32[64,2048]{1,0:T(8,128)}, f32[64,2048]{1,0:T(8,128)}, f32[64,2048]{1,0:T(8,128)}, f32[64,2048]{1,0:T(8,128)}, f32[64,5632]{1,0:T(8,128)}, /*index=5*/f32[64,5632]{1,0:T(8,128)}, f32[64,512]{1,0:T(8,128)}) custom-call(bf16[2048,384]{1,0:T(8,128)(2,1)} %copy.107.refs_0_, bf16[2048,384]{1,0:T(8,128)(2,1)} %copy.108.refs_1_, ...), custom_call_target="tpu_custom_call" | custom-call | tf_op jit(solution)/shard_map/pallas_call | solution.py:523
  1035.7 5.4 multiply_add_fusion
  1041.1 16.2 %convolution_add_fusion = f32[384,2048]{1,0:T(8,128)} fusion(f32[384,2048]{1,0:T(8,128)S(1)} %copy-done.7, bf16[384,5632]{1,0:T(8,128)(2,1)} %multiply_convert_fusion.2, bf16[5632,2048]{1,0:T(8,128)(2,1)} %all-gather.4.cloned.1.call-done), kind=kOutput, calls=%fused_computation.47 | convolution fusion | flops 8859156480 | bytes 33685504 | tf_op jit(solution)/shard_map/dot_general | solution.py:31
  (117 shorter events, 35.0 us)
Async XLA Ops:
  7.2 476.7 %all-gather.4.cloned.1.call-start = ((), (), s32[]{:S(2)}) async-start(), calls=%async_computation.1 | async-start | bytes 23789568 | tf_op jit(solution)/shard_map/all_gather | solution.py:704
  10.6 326.9 %copy-start.22 = (s32[3,1,128]{2,1,0:T(1,128)S(1)}, s32[3,1,128]{2,1,0:T(1,128)}, u32[]{:S(2)}) copy-start(s32[3,1,128]{2,1,0:T(1,128)} %param.15) | copy-start | bytes 4612
  10.6 329.3 %copy-start = (f32[3,1,128,2048]{3,2,1,0:T(8,128)S(1)}, f32[3,1,128,2048]{3,2,1,0:T(8,128)}, u32[]{:S(2)}) copy-start(f32[3,1,128,2048]{3,2,1,0:T(8,128)} %param.14) | copy-start | bytes 9437188
  337.5 719.8 %reduce-scatter.2.cloned.1.call-start = ((), (), s32[]{:S(2)}) async-start(), calls=%async_computation.2 | async-start | bytes 23789568 | tf_op jit(solution)/shard_map/reduce_scatter | solution.py:708
  337.6 24.4 %collective-permute-start = (s32[3,1]{1,0:T(4,128)S(1)}, s32[3,1]{1,0:T(4,128)S(1)}, u32[]{:S(2)}, u32[]{:S(2)}) collective-permute-start(s32[3,1]{1,0:T(4,128)S(1)} %slice.152), channel_id=1, source_target_pairs={{0,1},{1,2},{2,3},{3,4},{4,5},{5,6},{6,7},{8,9},{9,10},{10,11},{11... | collective-permute-start | bytes 44 | tf_op jit(solution)/shard_map/ppermute | solution.py:764
  339.9 1.9 copy-start.3
  341.8 1.7 copy-start.17
  362.1 10.8 %copy-start.19 = (f32[384]{0:T(512)}, f32[384]{0:T(512)S(1)}, u32[]{:S(2)}) copy-start(f32[384]{0:T(512)S(1)} %fusion.36) | copy-start | bytes 4612
  391.4 7.9 slice-start
  391.4 0.8 copy-start.10
  392.3 7.0 slice-start.1
  396.2 3.1 copy-start.1
  399.2 5.2 copy-start.9
  551.4 5.1 copy-start.4
  551.4 5.1 copy-start.6
  551.4 10.1 slice-start.2
  556.5 5.0 slice-start.3
  561.5 7.7 copy-start.8
  577.3 28.1 %copy-start.5 = (f32[3,128,2048]{2,1,0:T(8,128)S(1)}, f32[3,128,2048]{2,1,0:T(8,128)}, u32[]{:S(2)}) copy-start(f32[3,128,2048]{2,1,0:T(8,128)} %pad_maximum_fusion.1) | copy-start | bytes 9437188
  577.3 28.2 %copy-start.20 = (f32[384]{0:T(512)S(1)}, f32[384]{0:T(512)}, u32[]{:S(2)}) copy-start(f32[384]{0:T(512)} %copy-done.19) | copy-start | bytes 4612
  612.7 4.1 copy-start.2
  612.7 4.1 copy-start.18
  612.7 4.1 copy-start.21
  1035.7 5.4 copy-start.7
  1041.1 18.8 %copy-start.16 = (f32[64,2048]{1,0:T(8,128)S(1)}, f32[64,2048]{1,0:T(8,128)}, u32[]{:S(2)}) copy-start(f32[64,2048]{1,0:T(8,128)} %get-tuple-element.182) | copy-start | bytes 1572868
  1057.2 3.4 copy-start.15
  1057.2 4.2 copy-start.14
  1057.3 5.0 copy-start.13
  1057.3 5.7 copy-start.12
  1060.6 3.5 copy-start.11
Sparse Core Ops, SparseCore 0:
  337.6 146.2 all-gather.3
  486.2 279.0 reduce-scatter.1

commit v5 on v4

--- a/solution.py
+++ b/solution.py
@@ -211,24 +211,71 @@
     pl.semaphore_wait(barrier, len(peers))
 
 
-def scatter_kernel(dims, depth, wide, pairs, spans, has_vec, *refs):
+def scatter_kernel(dims, depth, wide, sides, spans, *refs):
     Y, X, Z = dims
     half = wide // 2
     f32, low = jnp.float32, jnp.bfloat16
     refs = list(refs)
     take = lambda n: [refs.pop(0) for _ in range(n)]
-    lefts, rights = take(pairs), take(pairs)
-    vec = take(1)[0] if has_vec else None
+    pairs, left_count = len(sides), max(sides) + 1
+    far_lefts, far_rights = take(left_count), take(pairs)
+    far_act, job_weight, far_base, vec = take(4)
     outs = take(len(spans))
+    (job_out,) = take(1)
+    lefts, rights = take(left_count), take(pairs)
+    act, slab, load_sem, slab_sem = take(4)
     (part, core_in, one_a, one_b, in_a, in_b, two_a, two_b, far_a, far_b, three, line_in) = take(12)
     (mid_a, mid_b, four_a, four_b, last_a, last_b) = take(6)
     (core_s, core_r, ya_s, ya_r, xb_s, xb_r, xa_s, xa_r, yb_s, yb_r, z_s, z_r) = take(12)
     (ma_s, ma_r, mb_s, mb_r, la_s, la_r, lb_s, lb_r) = take(8)
     (core_f, ya_f, xb_f, xa_f, yb_f, z_f, ma_f, mb_f, la_f, lb_f) = take(10)
+    sources = [far_lefts[0], far_rights[0], far_act, far_base] + far_lefts[1:] + far_rights[1:]
+    targets = [lefts[0], rights[0], act, job_out] + lefts[1:] + rights[1:]
+    loads = [
+        pltpu.make_async_copy(source, target, load_sem.at[n])
+        for n, (source, target) in enumerate(zip(sources, targets))
+    ]
+    for load in loads:
+        load.start()
     here = locate(dims)
     y, x, z, c = here
     greet(dims, here)
     total = spans[-1][2]
+    left_loads = [loads[0]] + loads[4 : 3 + left_count]
+    right_loads = [loads[1]] + loads[3 + left_count :]
+    slab_rows = slab.shape[1]
+    slabs = job_weight.shape[0] // slab_rows
+
+    def fetch(k):
+        rows = pl.ds(pl.multiple_of(k * slab_rows, slab_rows), slab_rows)
+        s = lax.rem(k, 2)
+        return pltpu.make_async_copy(job_weight.at[rows], slab.at[s], slab_sem.at[s])
+
+    def job(k):
+        @pl.when(k == -1)
+        def _():
+            fetch(0).start()
+
+        @pl.when(k == 0)
+        def _():
+            loads[2].wait()
+            loads[3].wait()
+
+        @pl.when(jnp.logical_and(k >= 0, k < slabs))
+        def _():
+            @pl.when(k + 1 < slabs)
+            def _():
+                fetch(k + 1).start()
+
+            fetch(k).wait()
+            s = lax.rem(k, 2)
+            depths = pl.ds(pl.multiple_of(k * slab_rows, slab_rows), slab_rows)
+            for first in range(0, job_out.shape[1], wide):
+                job_out[:, first : first + wide] += jnp.dot(
+                    act[:, depths],
+                    slab[s, :, first : first + wide],
+                    preferred_element_type=f32,
+                )
 
     def send(src, dst, ss, rs, peer):
         return pltpu.make_async_remote_copy(
@@ -328,6 +375,13 @@
         s = lax.rem(t, SLOTS)
         for pair in range(pairs):
             low_t, high_t = rights_span[pair]
+            left = lefts[sides[pair]]
+
+            @pl.when(t == low_t)
+            def _():
+                right_loads[pair].wait()
+                if sides.index(sides[pair]) == pair:
+                    left_loads[sides[pair]].wait()
 
             @pl.when(jnp.logical_and(t >= low_t, t < high_t))
             def _():
@@ -337,7 +391,7 @@
                     rows = Z * 2 * depth
                     first = pl.multiple_of(i * rows, rows)
                     value = jnp.dot(
-                        lefts[pair][pl.ds(first, rows), :],
+                        left[pl.ds(first, rows), :],
                         rights[pair][:, columns],
                         preferred_element_type=f32,
                     ).astype(low)
@@ -348,21 +402,19 @@
 
                 lax.fori_loop(0, Y * X, block, 0)
 
-        if has_vec:
-
-            @pl.when(t == total - 1)
-            def _():
-                def block(i, _):
-                    rows = Z * 2 * depth
-                    first = pl.multiple_of(i * rows, rows)
-                    value = vec[pl.ds(first, rows), :].reshape(Z, 2, depth, vec.shape[1])
-                    for core in range(2):
-                        part[s, core, lax.div(i, X), lax.rem(i, X), :, :, : vec.shape[1]] = value[
-                            :, core
-                        ]
-                    return 0
-
-                lax.fori_loop(0, Y * X, block, 0)
+        @pl.when(t == total - 1)
+        def _():
+            def block(i, _):
+                rows = Z * 2 * depth
+                first = pl.multiple_of(i * rows, rows)
+                value = vec[pl.ds(first, rows), :].reshape(Z, 2, depth, vec.shape[1])
+                for core in range(2):
+                    part[s, core, lax.div(i, X), lax.rem(i, X), :, :, : vec.shape[1]] = value[
+                        :, core
+                    ]
+                return 0
+
+            lax.fori_loop(0, Y * X, block, 0)
 
     rights_span = []
     start = 0
@@ -376,6 +428,8 @@
         def _():
             produce(t)
             begin(core_copies(t), t)
+
+        job(t - 2)
 
         u = t - 2
 
@@ -479,23 +533,30 @@
     lax.fori_loop(0, total + 8, step, 0)
 
 
-def scatter_call(dims, depth, wide, pairs, widths, vec, collective_id):
+def scatter_call(dims, depth, wide, lefts, sides, rights, widths, vec, job, collective_id):
     Y, X, Z = dims
     half = wide // 2
     low = jnp.bfloat16
-    widths = list(widths)
-    if vec is not None:
-        widths.append(wide)
+    widths = list(widths) + [wide]
     spans, start = [], 0
     for n in widths:
         spans.append((n, start, start + n // wide))
         start += n // wide
-    operands = [a for a, _ in pairs] + [b for _, b in pairs] + ([vec] if vec is not None else [])
+    act, weight, base = job
+    slab_rows = wide
+    assert weight.shape[0] % slab_rows == 0 and weight.shape[0] // slab_rows + 2 < start
+    operands = list(lefts) + list(rights) + [act, weight, base, vec]
     vmem = lambda *shape: pltpu.VMEM((SLOTS,) + shape, low)
     dma = lambda *shape: pltpu.SemaphoreType.DMA((SLOTS,) + shape)
     reg = lambda n: pltpu.SemaphoreType.REGULAR((n,))
     y1, x1, z1 = max(Y - 1, 1), max(X - 1, 1), max(Z - 1, 1)
-    scratch = [
+    scratch = [pltpu.VMEM(a.shape, a.dtype) for a in list(lefts) + list(rights) + [act]]
+    scratch += [
+        pltpu.VMEM((2, slab_rows, weight.shape[1]), weight.dtype),
+        pltpu.SemaphoreType.DMA((len(operands) - 2,)),
+        pltpu.SemaphoreType.DMA((2,)),
+    ]
+    scratch += [
         vmem(2, Y, X, Z, depth, wide),
         vmem(Y, X, Z, depth, wide),
         vmem(Y, X, Z, depth, half),
@@ -521,12 +582,12 @@
     scratch += [reg(1), reg(y1), reg(x1), reg(x1), reg(y1), reg(z1)]
     scratch += [reg(z1), reg(z1), reg(x1), reg(y1)]
     return pl.pallas_call(
-        functools.partial(
-            scatter_kernel, dims, depth, wide, len(pairs), spans, vec is not None
-        ),
-        out_shape=[jax.ShapeDtypeStruct((depth, n), jnp.float32) for n in widths],
-        in_specs=[pl.BlockSpec(memory_space=pltpu.VMEM)] * len(operands),
-        out_specs=[pl.BlockSpec(memory_space=pltpu.VMEM)] * len(widths),
+        functools.partial(scatter_kernel, dims, depth, wide, tuple(sides), spans),
+        out_shape=[jax.ShapeDtypeStruct((depth, n), jnp.float32) for n in widths]
+        + [jax.ShapeDtypeStruct(base.shape, base.dtype)],
+        in_specs=[pl.BlockSpec(memory_space=pl.ANY)] * (len(operands) - 1)
+        + [pl.BlockSpec(memory_space=pltpu.VMEM)],
+        out_specs=[pl.BlockSpec(memory_space=pltpu.VMEM)] * (len(widths) + 1),
         scratch_shapes=scratch,
         compiler_params=pltpu.CompilerParams(
             collective_id=collective_id, has_side_effects=True, vmem_limit_bytes=60 * 2**20
@@ -801,15 +862,10 @@
     grad_dense = grad_flat.astype(jnp.bfloat16)
     down_part = contract_rows(activated, grad_dense).astype(jnp.bfloat16)
     down_full, down_part = lax.optimization_barrier((down_full, down_part))
-    block_out = (middle + dot(activated, down_full)).reshape(inputs.shape)
     grad_act = contract_last(grad_dense, down_full)
-    grad_up = jnp.concatenate(
-        [
-            (grad_act * up_two * silu_slope(up_one)).astype(jnp.bfloat16),
-            (grad_act * jax.nn.silu(up_one)).astype(jnp.bfloat16),
-        ],
-        axis=1,
-    )
+    grad_up_one = (grad_act * up_two * silu_slope(up_one)).astype(jnp.bfloat16)
+    grad_up_two = (grad_act * jax.nn.silu(up_one)).astype(jnp.bfloat16)
+    grad_up = jnp.concatenate([grad_up_one, grad_up_two], axis=1)
     grad_normed_two = contract_last(grad_up, up_full)
     gain_two = jnp.sum(grad_normed_two * scaled_two, axis=0)
     grad_middle = grad_flat + norm_back(grad_normed_two * dense_gain_all, scaled_two, scale_two)
@@ -855,16 +911,20 @@
     vector_sums = jnp.stack([gain_one, floor_sum, gain_out, gain_two], axis=1)
     vector_sums = jnp.pad(vector_sums, ((0, 0), (0, LANES - 4))).astype(low)
     if own_kernel:
-        *grads, vector_terms = scatter_call(
+        *grads, vector_terms, block_out = scatter_call(
             dims,
             depth,
             wide,
-            [(normed_one.T, grad_pre), (mixed.T, grad_mixer), (normed_two.T, grad_up)],
+            [normed_one.T, mixed.T, normed_two.T],
+            [0, 0, 0, 1, 2, 2],
+            [grad_pre_input, grad_pre_forget, grad_pre_gate, grad_mixer, grad_up_one, grad_up_two],
             [width] * 4 + [hidden] * 2,
             vector_sums,
+            (activated, down_full, middle),
             1,
         )
     else:
+        block_out = middle + dot(activated, down_full)
         terms = scatter_all(
             jnp.concatenate(
                 [
@@ -881,7 +941,7 @@
         *grads, vector_terms = jnp.split(terms, marks, axis=1)
     down_grad = scatter_all(down_part).astype(jnp.float32)
     return (
-        block_out,
+        block_out.reshape(inputs.shape),
         input_grad,
         vector_terms[:, 0],
         grads[0],

time: 1080 us -> 1060 us (0.981)
  other arithmetic: 82.6 us -> 67.5 us
  Pallas kernels: 722 us -> 736 us
  matrix products: 163 us -> 150 us
    dot_general x4 -> x3, matrix products: 68.9 us -> 52.8 us  [dot(): return jnp.dot(left, right, preferred_element_type=jnp.float32)]
    pallas_call x1, Pallas kernels: 379 us -> 394 us  [scatter_call(): pl.pallas_call(functools.partial(scatter_kernel, dims, depth, wide, tuple...]
    concatenate x2 -> x0, other arithmetic: 13.6 us -> none  [the longest x1 7.85 us: shards(): jnp.concatenate([(grad_act * up_two * silu_slope(up_one)).astype(jnp.bflo...]
  transfers between devices with their start and end apart: 3 -> 3, of which waited for: 1 -> 1; matrix products, arithmetic and copies ran while one was open for 24% -> 21% of each run, Pallas kernels for 37% -> 39%
where the time goes in v5:
time: 1060 us; the launch traced here: 1050 us
  Pallas kernels  736 us (69%)
  matrix products  150 us (14%)
  other arithmetic  67.5 us (6%)
  blocking collectives  32 us (3%)
  local copies, waits for them, and re-layouts  28.5 us (3%)
  waiting for transfers between devices  21.9 us (2%)
  between operations  14.9 us (1%)
    pallas_call x1, Pallas kernels, scatter_call(): pl.pallas_call(functools.partial(scatter_kernel, dims, depth, wide, tuple...  394 us
    pallas_call x1, Pallas kernels, gather_call(): pl.pallas_call(functools.partial(gather_kernel, dims, wides), out_shape=[...  321 us
    dot_general x4, matrix products, contract_last(): lax.dot_general(left, right, (((1,), (1,)), ((), ())), preferred_element_...  79.9 us
    dot_general x3, matrix products, dot(): return jnp.dot(left, right, preferred_element_type=jnp.float32)  52.8 us
    all_gather x2, blocking collectives, exchange(): return lax.all_gather(value.astype(jnp.bfloat16), 'seq').astype(jnp.float32)  32 us
    all_gather x1, waiting for transfers between devices, gather_all(): return lax.all_gather(shard, ALL, axis=0, tiled=True)  21.8 us
  transfers between devices with their start and end apart: 3, of which 1 were waited for; matrix products, arithmetic and copies ran while one was open for 21% of the time, Pallas kernels for 39%

profile of v5, /device:TPU:0, one launch (start us, length us, event | category | flops | bytes accessed | tf_op | source)
XLA Modules:
  0.0 1054.0 jit_solution(9983007887400295293)
XLA Ops:
  8.1 2.5 pad_maximum_fusion.1.refs_2_
  10.6 2.2 fusion.20.refs_0_
  12.8 320.9 %shard_map.237 = (bf16[2,2,4,2,64,6400]{5,4,3,2,1,0:T(8,128)(2,1)}, bf16[2,2,4,2,64,2048]{5,4,3,2,1,0:T(8,128)(2,1)}, bf16[2,2,4,2,64,11264]{5,4,3,2,1,0:T(8,128)(2,1)}) custom-call(bf16[64,6400]{1,0:T(8,128)(2,1)} %fusion.20.refs_0_, bf16[64,2048]{1,0:T(8,128)(2,1)} %refs_1_.1, bf16[64,11264]{1,0:T(8,128)(2,1)} %pad_maximum_fusion.1.refs_2_), custom_call_target="tpu_custom_call" | custom-call | tf_op jit(solution)/shard_map/pallas_call | solution.py:743
  337.0 2.3 collective-permute-start
  342.9 18.3 %fusion.60.refs_0_.refs_1_ = f32[384,6400]{1,0:T(8,128)} fusion(bf16[384,2048]{1,0:T(8,128)(2,1)S(1)} %bitcast.386, bf16[2048,6400]{1,0:T(8,128)(2,1)} %bitcast.402), kind=kOutput, calls=%fused_computation.167 | convolution fusion | flops 10066329600 | bytes 37617664 | tf_op jit(solution)/shard_map/dot_general | solution.py:31
  362.1 10.0 shard_map.238
  374.1 17.3 %all_gather.13 = bf16[8,6,2048]{2,1,0:T(8,128)(2,1)S(1)} all-gather(bf16[1,6,2048]{2,1,0:T(8,128)(2,1)S(1)} %pad_maximum_fusion.2), channel_id=1, replica_groups=mesh['dp'=4,'seq'=8] {'seq'}, dimensions={0}, use_global_device_ids=true | all-gather | bytes 221184 | tf_op jit(solution)/shard_map/all_gather | solution.py:163
  392.3 3.9 multiply_reduce_fusion.7
  396.2 4.0 multiply_convert_fusion.7
  400.4 5.2 multiply_reduce_fusion.6
  405.5 29.4 %fusion.53 = f32[384,11264]{1,0:T(8,128)} fusion(bf16[2048,11264]{1,0:T(8,128)(2,1)} %bitcast.408, f32[384,2048]{1,0:T(8,128)} %get-tuple-element.163.refs_11_, f32[2048]{0:T(1024)S(1)} %bitcast.396, f32[384]{0:T(512)S(1)} %add_rsqrt_fusion), kind=kOutput, calls=%fused_computation.163 | convolution fusion | flops 17719099392 | bytes 66594304 | tf_op jit(solution)/shard_map/dot_general | solution.py:31
  434.9 9.5 multiply_convert_fusion.2.refs_9_
  444.4 17.6 %convolution_convert_fusion = bf16[5632,2048]{1,0:T(8,128)(2,1)} fusion(bf16[384,5632]{1,0:T(8,128)(2,1)} %multiply_convert_fusion.2.refs_9_, bf16[384,2048]{1,0:T(8,128)(2,1)S(1)} %copy-done.11), kind=kOutput, calls=%fused_computation | convolution fusion | flops 8869904384 | bytes 28966912 | tf_op jit(solution)/shard_map/dot_general | solution.py:41
  462.0 21.8 %all-gather.4.cloned.1.call-done.refs_10_ = bf16[5632,2048]{1,0:T(8,128)(2,1)} async-done(((bf16[176,2048]{1,0:T(8,128)(2,1)}), bf16[5632,2048]{1,0:T(8,128)(2,1)}) %all-gather.4.cloned.1.call-update) | async-done | bytes 23068688 | tf_op jit(solution)/shard_map/all_gather | solution.py:765
  483.9 2.8 copy.108.refs_1_
  488.9 2.9 slice_add_fusion
  493.8 22.5 %multiply_convert_fusion.1 = (bf16[384,5632]{1,0:T(8,128)(2,1)}, bf16[384,5632]{1,0:T(8,128)(2,1)}) fusion(f32[384,11264]{1,0:T(8,128)} %fusion.53, bf16[5632,2048]{1,0:T(8,128)(2,1)} %all-gather.4.cloned.1.call-done.refs_10_, bf16[384,2048]{1,0:T(8,128)(2,1)} %bitcast_convert_fusion), kind=kOutput, calls=%fused_computation.7 | convolution fusion | flops 8886484992 | bytes 50593792 | tf_op jit(solution)/shard_map/dot_general | solution.py:35
  516.3 26.9 %multiply_reduce_fusion.1 = (bf16[2048]{0:T(1024)(128)(2,1)S(1)}, f32[384]{0:T(512)S(1)}, f32[384,2048]{1,0:T(8,128)}) fusion(f32[384,2048]{1,0:T(8,128)S(1)} %copy-done.6, f32[384]{0:T(512)S(1)} %add_rsqrt_fusion, f32[2048]{0:T(1024)S(1)} %bitcast.397, bf16[2048,11264]{1,0:T(8,128)(2,1)} %bitcast.409, bf16[384,5632]{1,0:T(8,128)(2,1)} %get-tuple-element.150.refs_8_, ...), kind=kOutput, calls=%fused_computation.35 | convolution fusion | flops 17738758144 | bytes 61094912 | tf_op jit(solution)/shard_map/dot_general | solution.py:35
  543.3 7.2 fusion.58
  550.5 11.8 %multiply_reduce_fusion.2 = (bf16[2048]{0:T(1024)(128)(2,1)S(1)}, f32[384]{0:T(512)S(1)}, bf16[384,2048]{1,0:T(8,128)(2,1)}, f32[384,2048]{1,0:T(8,128)}) fusion(f32[384,2048]{1,0:T(8,128)S(1)} %copy-done.3, f32[384]{0:T(512)S(1)} %copy-done.23, f32[384,6400]{1,0:T(8,128)} %fusion.60.refs_0_.refs_1_, f32[2048]{0:T(1024)S(1)} %bitcast.393, ...), kind=kOutput, calls=%fused_computation.36 | convolution fusion | flops 3236165120 | bytes 20986880 | tf_op jit(solution)/shard_map/dot_general | solution.py:35
  562.3 2.6 copy.109.refs_2_
  564.9 5.8 subtract_multiply_fusion.refs_0_
  570.8 11.4 %shard_map.239 = (f32[384,2048]{1,0:T(8,128)}, f32[384,2048]{1,0:T(8,128)}, f32[3,2048]{1,0:T(4,128)}) custom-call(f32[384,2048]{1,0:T(8,128)} %subtract_multiply_fusion.refs_0_, f32[384,6400]{1,0:T(8,128)} %fusion.60.refs_0_.refs_1_, f32[1,2048]{1,0:T(1,128)} %get-tuple-element.158.refs_2_, f32[384,128]{1,0:T(8,128)} %broadcast_in_dim.9.refs_3_), custom_call_target="tpu_custom_call" | custom-call | tf_op jit(solution)/shard_map/pallas_call | solution.py:147
  582.9 14.7 %all-gather.1 = bf16[8,3,2048]{2,1,0:T(4,128)(2,1)S(1)} all-gather(bf16[1,3,2048]{2,1,0:T(4,128)(2,1)S(1)} %convert_bitcast_fusion), channel_id=2, replica_groups=mesh['dp'=4,'seq'=8] {'seq'}, dimensions={0}, use_global_device_ids=true | all-gather | bytes 110592 | tf_op jit(solution)/shard_map/all_gather | solution.py:163
  598.8 7.5 fusion.55
  606.2 4.1 multiply_convert_fusion.4.refs_4_
  610.4 18.8 %multiply_reduce_fusion = (f32[384]{0:T(512)S(1)}, bf16[2048]{0:T(1024)(128)(2,1)S(1)}, f32[384,2048]{1,0:T(8,128)}) fusion(f32[3,1,128,2048]{3,2,1,0:T(8,128)S(1)} %copy-done.1, f32[2048]{0:T(1024)S(1)} %bitcast.390, f32[384]{0:T(512)S(1)} %copy-done.26, bf16[2048,6400]{1,0:T(8,128)(2,1)} %bitcast.403, bf16[384,2048]{1,0:T(8,128)(2,1)} %get-tuple-element.152.refs_5_, ...), kind=kOutput, calls=%fused_computation.34 | convolution fusion | flops 10090706944 | bytes 37252608 | tf_op jit(solution)/shard_map/dot_general | solution.py:35
  629.2 6.0 multiply_add_fusion
  635.2 2.6 copy.107.refs_0_
  639.0 394.1 %shard_map.240 = (f32[64,2048]{1,0:T(8,128)}, f32[64,2048]{1,0:T(8,128)}, f32[64,2048]{1,0:T(8,128)}, f32[64,2048]{1,0:T(8,128)}, f32[64,5632]{1,0:T(8,128)}, /*...) custom-call(bf16[2048,384]{1,0:T(8,128)(2,1)} %copy.107.refs_0_, bf16[2048,384]{1,0:T(8,128)(2,1)} %copy.108.refs_1_, ...), custom_call_target="tpu_custom_call" | custom-call | tf_op jit(solution)/shard_map/pallas_call | solution.py:584
  1034.8 2.4 convert_element_type.98
  1037.2 4.1 copy.140
  (119 shorter events, 26.1 us)
Async XLA Ops:
  7.2 476.6 %all-gather.4.cloned.1.call-start = ((), (), s32[]{:S(2)}) async-start(), calls=%async_computation.1 | async-start | bytes 23789568 | tf_op jit(solution)/shard_map/all_gather | solution.py:765
  10.6 326.3 %copy-start.27 = (s32[3,1,128]{2,1,0:T(1,128)S(1)}, s32[3,1,128]{2,1,0:T(1,128)}, u32[]{:S(2)}) copy-start(s32[3,1,128]{2,1,0:T(1,128)} %param.15) | copy-start | bytes 4612
  10.6 328.8 %copy-start = (f32[3,1,128,2048]{3,2,1,0:T(8,128)S(1)}, f32[3,1,128,2048]{3,2,1,0:T(8,128)}, u32[]{:S(2)}) copy-start(f32[3,1,128,2048]{3,2,1,0:T(8,128)} %param.14) | copy-start | bytes 9437188
  336.9 698.0 %reduce-scatter.2.cloned.1.call-start = ((), (), s32[]{:S(2)}) async-start(), calls=%async_computation.2 | async-start | bytes 23789568 | tf_op jit(solution)/shard_map/reduce_scatter | solution.py:769
  337.0 24.2 %collective-permute-start = (s32[3,1]{1,0:T(4,128)S(1)}, s32[3,1]{1,0:T(4,128)S(1)}, u32[]{:S(2)}, u32[]{:S(2)}) collective-permute-start(s32[3,1]{1,0:T(4,128)S(1)} %slice.152), channel_id=1, source_target_pairs={{0,1},{1,2},{2,3},{3,4},{4,5},{5,6},{6,7},{8,9},{9,10},{10,11},{11... | collective-permute-start | bytes 44 | tf_op jit(solution)/shard_map/ppermute | solution.py:825
  339.3 1.9 copy-start.7
  341.2 1.7 copy-start.18
  341.2 55.0 %copy-start.20 = (f32[1,2048]{1,0:T(1,128)}, f32[1,2048]{1,0:T(1,128)S(1)}, u32[]{:S(2)}) copy-start(f32[1,2048]{1,0:T(1,128)S(1)} %get-tuple-element.157) | copy-start | bytes 24580
  361.3 10.8 %copy-start.24 = (f32[384]{0:T(512)}, f32[384]{0:T(512)S(1)}, u32[]{:S(2)}) copy-start(f32[384]{0:T(512)S(1)} %fusion.48) | copy-start | bytes 4612
  391.4 8.9 slice-start
  392.3 8.0 slice-start.1
  396.2 4.1 copy-start.2
  396.2 4.1 copy-start.22
  400.3 5.2 copy-start.9
  434.9 9.5 copy-start.11
  483.8 5.0 copy-start.4
  493.8 22.5 %copy-start.6 = (f32[384,2048]{1,0:T(8,128)S(1)}, f32[384,2048]{1,0:T(8,128)}, u32[]{:S(2)}) copy-start(f32[384,2048]{1,0:T(8,128)} %get-tuple-element.163.refs_11_) | copy-start | bytes 9437188
  543.2 7.3 copy-start.3
  543.3 7.3 copy-start.21
  543.3 7.3 copy-start.23
  550.5 11.8 %copy-start.8 = (bf16[384,2048]{1,0:T(8,128)(2,1)}, bf16[384,2048]{1,0:T(8,128)(2,1)S(1)}, u32[]{:S(2)}) copy-start(bf16[384,2048]{1,0:T(8,128)(2,1)S(1)} %get-tuple-element.145.refs_6_) | copy-start | bytes 4718596
  570.8 28.0 %copy-start.5 = (f32[3,128,2048]{2,1,0:T(8,128)S(1)}, f32[3,128,2048]{2,1,0:T(8,128)}, u32[]{:S(2)}) copy-start(f32[3,128,2048]{2,1,0:T(8,128)} %pad_maximum_fusion) | copy-start | bytes 9437188
  570.8 28.0 %copy-start.25 = (f32[384]{0:T(512)S(1)}, f32[384]{0:T(512)}, u32[]{:S(2)}) copy-start(f32[384]{0:T(512)} %copy-done.24) | copy-start | bytes 4612
  606.2 4.1 copy-start.1
  606.2 4.1 copy-start.19
  606.2 4.1 copy-start.26
  1037.2 4.1 copy-start.17
  1037.2 4.9 copy-start.16
  1037.2 5.7 copy-start.15
  1037.2 6.5 copy-start.14
  1041.3 3.2 copy-start.13
  1042.1 3.5 copy-start.12
  (1 other events, 0.8 us)
Sparse Core Ops, SparseCore 0:
  337.0 146.7 all-gather.3
  486.1 314.2 reduce-scatter.1
